TPU v7x, 128 devices: a whole 4x4x4 slice. The times are simulated.
128 devices in a mesh: sec: 2 (over core), col: 64 (over x, z, y).
Axes of the slice: x: 4, y: 4, z: 4, core: 2. Of those that a mesh axis runs over, the one named last changes fastest.
Arguments:
- gcm_state: bfloat16 [4, 72, 16384], P(None, None, ('sec', 'col')), may hold values from -6 to 6
- host_place: int32 [16384], P(('sec', 'col')), may hold values from 0 to 16383, as said below
- switch: int32 [16384], P(('sec', 'col')), may hold values 0 or 1
- coarse_to_fine_map: bfloat16 [60, 72], replicated, may hold values from -0.75 to 0.75
- pert_temp: bfloat16 [60, 64, 16384], P(None, None, ('sec', 'col')), may hold values from -6 to 6
- pert_moist: bfloat16 [60, 64, 16384], P(None, None, ('sec', 'col')), may hold values from -6 to 6
- fine_to_coarse_map: float32 [72, 60], replicated, may hold values from -0.75 to 0.75
- node_ids: int32 [4, 16384], P(None, ('sec', 'col')), may hold values from 0 to 16383, as said below
- dss_weight: float32 [4, 16384], P(None, ('sec', 'col')), may hold values from 0.25 to 1
Outputs:
- crm_temp: bfloat16 [60, 64, 16384], P(None, None, ('sec', 'col'))
- node_tend: float32 [3, 72, 16384], P(None, None, ('sec', 'col'))
Inputs may be any that keep to these rules, and one draw needn't show every extreme that they name: A permutation: the embedded model of column j is at position host_place[j]; positions d * 128 to (d + 1) * 128 - 1 belong to device d. Of the columns of one device at most 2 have positions on any one device, and 2 is reached. `node_ids`: nodes d * 128 to (d + 1) * 128 - 1 belong to device d. Of the 512 entries at positions of one device, at most 8 name nodes of any one device, and 8 is reached.
All inputs are finite; a program needn't handle non-finite values. No bound on the sum of `switch` on one device may be relied on, other than what follows from the above.
Results may differ from a plain program's by a relative error of at most 0.001.
Values may be sent and summed in bfloat16 or wider, within the bound.
A program may use at most 64 MiB of HBM per device.

v0:
```python
import jax
import jax.numpy as jnp
from jax import lax
from jax.sharding import PartitionSpec as P

SUB = 4


relax_rate = 0.3
vapor_capacity_offset = 0.5
vapor_capacity_gradient = 0.3
vapor_release_factor = 1.5
rainfall_flux = 0.5


def flux_divergence_term(field, lateral_stability_factor, upward_stability_factor, target):
    left_cells = jnp.roll(field, 1, axis=1)
    right_cells = jnp.roll(field, -1, axis=1)
    field = (
        field
        - jnp.maximum(lateral_stability_factor, 0.0) * (field - left_cells)
        - jnp.minimum(lateral_stability_factor, 0.0) * (right_cells - field)
    )
    below = jnp.concatenate([field[:1], field[:-1]], axis=0)
    above = jnp.concatenate([field[1:], field[-1:]], axis=0)
    field = (
        field
        - jnp.maximum(upward_stability_factor, 0.0) * (field - below)
        - jnp.minimum(upward_stability_factor, 0.0) * (above - field)
    )
    return field + relax_rate * (target[:, None, :] - jnp.mean(field, axis=1, keepdims=True))


def inner_resolved_solver(
    solver_conditions, indicator_bits, coarse_to_fine_map, thermal_deviation, moisture_deviation
):
    levels = coarse_to_fine_map.shape[1]
    count = solver_conditions.shape[1]
    stacked = solver_conditions.reshape(4, levels, count)
    height_distribution = jnp.einsum(
        "kl,vlp->vkp", coarse_to_fine_map, stacked, preferred_element_type=jnp.float32
    )
    lateral_stability_factor = (0.45 * jnp.tanh(height_distribution[0]))[:, None, :]
    upward_stability_factor = (0.3 * jnp.tanh(height_distribution[1]))[:, None, :]
    thermal_state_kelvin = height_distribution[2][:, None, :] + thermal_deviation.astype(
        jnp.float32
    )
    vapor_mass_fraction = height_distribution[3][:, None, :] + moisture_deviation.astype(
        jnp.float32
    )
    initial_thermal_state = thermal_state_kelvin
    initial_vapor_fraction = vapor_mass_fraction
    phase_change_mass = jnp.zeros_like(thermal_state_kelvin)
    sentinel_entry = indicator_bits.astype(jnp.float32)[None, None, :]
    for substep in range(SUB):
        thermal_state_kelvin = flux_divergence_term(
            thermal_state_kelvin,
            lateral_stability_factor,
            upward_stability_factor,
            height_distribution[2],
        )
        vapor_mass_fraction = flux_divergence_term(
            vapor_mass_fraction,
            lateral_stability_factor,
            upward_stability_factor,
            height_distribution[3],
        )
        liquid_condensate_grid = (
            sentinel_entry
            * rainfall_flux
            * jnp.maximum(
                vapor_mass_fraction
                - vapor_capacity_offset * jnp.exp(vapor_capacity_gradient * thermal_state_kelvin),
                0.0,
            )
        )
        vapor_mass_fraction = vapor_mass_fraction - liquid_condensate_grid
        thermal_state_kelvin = thermal_state_kelvin + vapor_release_factor * liquid_condensate_grid
        phase_change_mass = phase_change_mass + liquid_condensate_grid
    forcing_grid = jnp.stack(
        [
            jnp.mean(thermal_state_kelvin - initial_thermal_state, axis=1),
            jnp.mean(vapor_mass_fraction - initial_vapor_fraction, axis=1),
            jnp.mean(phase_change_mass, axis=1),
        ]
    )
    return (thermal_state_kelvin.astype(jnp.bfloat16), forcing_grid)


def slot_ranks(destination, device_count):
    one_hot = (destination[:, None] == jnp.arange(device_count)[None, :]).astype(jnp.int32)
    before = jnp.cumsum(one_hot, axis=0) - one_hot
    return jnp.sum(before * one_hot, axis=1)


def body(
    gcm_state,
    host_place,
    switch,
    coarse_to_fine_map,
    pert_temp,
    pert_moist,
    fine_to_coarse_map,
    node_ids,
    dss_weight,
):
    per_dev = host_place.shape[0]
    levels = gcm_state.shape[1]
    sections = lax.axis_size("sec")
    column_groups = lax.axis_size("col")
    device_count = sections * column_groups
    capacity = 2 * per_dev // device_count
    span = device_count * capacity
    destination = host_place // per_dev
    slot = destination * capacity + slot_ranks(destination, device_count)
    flat_states = gcm_state.reshape(4 * levels, per_dev)
    outgoing = jnp.zeros((4 * levels, span), jnp.bfloat16).at[:, slot].set(flat_states)
    target_rows = jnp.full((span,), per_dev, jnp.int32).at[slot].set(host_place % per_dev)
    flag_slots = jnp.zeros((span,), jnp.int32).at[slot].set(switch)
    labels = jnp.stack([target_rows, flag_slots])
    received, got_labels = (
        lax.all_to_all(outgoing, ("sec", "col"), split_axis=1, concat_axis=1, tiled=True),
        lax.all_to_all(labels, ("sec", "col"), split_axis=1, concat_axis=1, tiled=True),
    )
    host_states = (
        jnp.zeros((4 * levels, per_dev + 1), jnp.bfloat16)
        .at[:, got_labels[0]]
        .set(received)[:, :per_dev]
    )
    host_flags = jnp.zeros((per_dev + 1,), jnp.int32).at[got_labels[0]].set(got_labels[1])[:per_dev]
    crm_temp, forcing_grid = inner_resolved_solver(
        host_states, host_flags, coarse_to_fine_map, pert_temp, pert_moist
    )
    sent_tend = jnp.einsum(
        "lk,vkp->vlp", fine_to_coarse_map, forcing_grid, precision=lax.Precision.HIGHEST
    )
    row_count = sent_tend.shape[0] * sent_tend.shape[1]
    capacity_node = 8 * per_dev // device_count
    span_node = device_count * capacity_node
    contrib = (dss_weight[None, :, :] * sent_tend.reshape(row_count, 1, per_dev)).reshape(
        row_count, 4 * per_dev
    )
    node_flat = node_ids.reshape(4 * per_dev)
    owner_device = node_flat // per_dev
    node_slot = owner_device * capacity_node + slot_ranks(owner_device, device_count)
    values_out = jnp.zeros((row_count, span_node), jnp.float32).at[:, node_slot].set(contrib)
    node_labels = (
        jnp.full((1, span_node), per_dev, jnp.int32).at[0, node_slot].set(node_flat % per_dev)
    )
    got_values, got_nodes = (
        lax.all_to_all(values_out, ("sec", "col"), split_axis=1, concat_axis=1, tiled=True),
        lax.all_to_all(node_labels, ("sec", "col"), split_axis=1, concat_axis=1, tiled=True),
    )
    node_sum = (
        jnp.zeros((row_count, per_dev + 1), jnp.float32)
        .at[:, got_nodes[0]]
        .add(got_values)[:, :per_dev]
    )
    return (crm_temp, node_sum.reshape(3, levels, per_dev))


def solution(mesh):
    return jax.shard_map(
        body,
        mesh=mesh,
        in_specs=(
            P(None, None, ("sec", "col")),
            P(("sec", "col")),
            P(("sec", "col")),
            P(),
            P(None, None, ("sec", "col")),
            P(None, None, ("sec", "col")),
            P(),
            P(None, ("sec", "col")),
            P(None, ("sec", "col")),
        ),
        out_specs=(P(None, None, ("sec", "col")), P(None, None, ("sec", "col"))),
        check_vma=False,
    )
```

profile of v0, /device:TPU:1, one launch (start us, length us, event | category | flops | bytes accessed | tf_op | source)
XLA Modules:
  0.0 128.1 jit_solution(10590073265582321246)
XLA Ops:
  2.9 1.1 scatter_custom_fusion.1
  5.0 11.5 %all-to-all-start = ((s32[2,128,2]{2,0,1:T(2,128)}), s32[2,128,2]{2,0,1:T(2,128)S(1)}, u32[]{:S(2)}, u32[]{:S(2)}) async-start(s32[2,128,2]{2,0,1:T(2,128)} %copy.32), calls=%async_computation | async-start | bytes 262144 | tf_op jit(solution)/shard_map/all_to_all | solution.py:123
  18.7 1.1 scatter_custom_fusion.2
  20.6 2.4 %scatter_custom_fusion.5 = s32[1024]{0:T(1024)S(1)} fusion(s32[512]{0:T(512)S(1)} %bitcast.124, s32[512]{0:T(512)S(1)} %get-tuple-element.126, s32[]{:T(128)} %constant.90.clone.1), kind=kCustom, calls=%fused_computation.201 | custom fusion | bytes 4100 | tf_op jit(solution)/shard_map/scatter | solution.py:148
  23.8 2.5 %all-to-all-done = s32[2,128,2]{2,0,1:T(2,128)S(1)} async-done(((s32[2,128,2]{2,0,1:T(2,128)}), s32[2,128,2]{2,0,1:T(2,128)S(1)}, u32[]{:S(2)}, u32[]{:S(2)}) %all-to-all-start) | async-done | bytes 2080 | tf_op jit(solution)/shard_map/all_to_all | solution.py:123
  26.3 7.2 %all-to-all-start.1 = ((bf16[288,128,2]{0,2,1:T(2,128)(2,1)}), bf16[288,128,2]{0,2,1:T(2,128)(2,1)S(1)}, u32[]{:S(2)}, u32[]{:S(2)}) async-start(bf16[288,128,2]{0,2,1:T(2,128)(2,1)} %all_to_all.27), calls=%async_computation.1 | async-start | bytes 393216 | tf_op jit(solution)/shard_map/all_to_all | solution.py:122
  34.2 1.4 %scatter_custom_fusion.4 = s32[129]{0:T(256)S(1)} fusion(s32[256]{0:T(256)S(1)} %bitcast.126, s32[256]{0:T(256)S(1)} %reshape.430, s32[]{:T(128)} %constant.92.clone.1), kind=kCustom, calls=%fused_computation.213 | custom fusion | bytes 520 | tf_op jit(solution)/shard_map/scatter | solution.py:130
  35.6 8.3 %all-to-all-done.1 = bf16[288,128,2]{0,2,1:T(2,128)(2,1)S(1)} async-done(((bf16[288,128,2]{0,2,1:T(2,128)(2,1)}), bf16[288,128,2]{0,2,1:T(2,128)(2,1)S(1)}, u32[]{:S(2)}, u32[]{:S(2)}) %all-to-all-start.1) | async-done | bytes 147488 | tf_op jit(solution)/shard_map/all_to_all | solution.py:122
  43.9 4.4 %all-to-all-start.2 = ((s32[1,128,8]{2,0,1:T(1,128)}), s32[1,128,8]{2,0,1:T(1,128)S(1)}, u32[]{:S(2)}, u32[]{:S(2)}) async-start(s32[1,128,8]{2,0,1:T(1,128)} %bitcast.20), calls=%async_computation.2 | async-start | bytes 131072 | tf_op jit(solution)/shard_map/all_to_all | solution.py:152
  48.5 1.5 %scatter_custom_fusion.3 = bf16[288,129]{0,1:T(8,128)(2,1)S(1)} fusion(s32[256]{0:T(256)S(1)} %bitcast.127, bf16[288,256]{0,1:T(8,128)(2,1)S(1)} %reshape.419, bf16[]{:T(256)} %constant.89.clone.1), kind=kCustom, calls=%fused_computation.135 | custom fusion | bytes 270914 | tf_op jit(solution)/shard_map/scatter | solution.py:128
  52.0 2.7 %fusion.10 = (f32[60,64,128]{2,1,0:T(8,128)S(1)}, f32[60,64,128]{2,1,0:T(8,128)S(1)}) fusion(f32[60,63,128]{2,1,0:T(8,128)S(1)} %get-tuple-element.85, f32[60,1,128]{2,1,0:T(1,128)S(1)} %get-tuple-element.87, f32[60,1,128]{2,1,0:T(1,128)S(1)} %get-tuple-element.86, f32[60,63,128]{2,1,0:T(8,128)S(1)} %get-tuple-element.84, ...), kind=kLoop, calls=%fused_computation.23 | loop fusion | flops 9830400 | bytes 13885440 | tf_op jit(solution)/shard_map/sub | solution.py:20
  55.8 2.5 %fusion.118 = (f32[60,128]{1,0:T(8,128)S(1)}, f32[60,64,128]{2,1,0:T(8,128)S(1)}, f32[60,128]{1,0:T(8,128)S(1)}, f32[60,64,128]{2,1,0:T(8,128)S(1)}) fusion(f32[60,64,128]{2,1,0:T(8,128)S(1)} %get-tuple-element.124, f32[1,64,128]{2,1,0:T(8,128)S(1)} %get-tuple-element.81, f32[59,64,128]{2,1,0:T(8,128)S(1)} %get-tuple-element.83, ...), kind=kLoop, calls=%fused_computation.226 | loop fusion | flops 8832000 | bytes 15851520 | tf_op jit(solution)/shard_map/reduce_sum | solution.py:31
  60.6 2.2 %fusion.26 = (f32[60,64,128]{2,1,0:T(8,128)S(1)}, f32[60,64,128]{2,1,0:T(8,128)S(1)}) fusion(f32[60,64,128]{2,1,0:T(8,128)S(1)} %get-tuple-element.30, f32[60,63,128]{2,1,0:T(8,128)S(1)} %get-tuple-element.69, f32[60,1,128]{2,1,0:T(1,128)S(1)} %get-tuple-element.71, f32[60,1,128]{2,1,0:T(1,128)S(1)} %get-tuple-element.70, ...), kind=kLoop, calls=%fused_computation.47 | loop fusion | flops 7864320 | bytes 15790080 | tf_op jit(solution)/shard_map/sub | solution.py:20
  63.8 2.5 %fusion.114 = (f32[60,128]{1,0:T(8,128)S(1)}, f32[60,64,128]{2,1,0:T(8,128)S(1)}, f32[60,128]{1,0:T(8,128)S(1)}, f32[60,64,128]{2,1,0:T(8,128)S(1)}) fusion(f32[60,64,128]{2,1,0:T(8,128)S(1)} %get-tuple-element.120, f32[1,64,128]{2,1,0:T(8,128)S(1)} %get-tuple-element.65, f32[59,64,128]{2,1,0:T(8,128)S(1)} %get-tuple-element.67, ...), kind=kLoop, calls=%fused_computation.224 | loop fusion | flops 8832000 | bytes 15851520 | tf_op jit(solution)/shard_map/reduce_sum | solution.py:31
  68.7 2.2 %fusion.42 = (f32[60,64,128]{2,1,0:T(8,128)S(1)}, f32[60,64,128]{2,1,0:T(8,128)S(1)}) fusion(f32[60,64,128]{2,1,0:T(8,128)S(1)} %get-tuple-element.28, f32[60,63,128]{2,1,0:T(8,128)S(1)} %get-tuple-element.53, f32[60,1,128]{2,1,0:T(1,128)S(1)} %get-tuple-element.55, f32[60,1,128]{2,1,0:T(1,128)S(1)} %get-tuple-element.54, ...), kind=kLoop, calls=%fused_computation.71 | loop fusion | flops 7864320 | bytes 15790080 | tf_op jit(solution)/shard_map/sub | solution.py:20
  71.9 2.7 %fusion.110 = (f32[60,128]{1,0:T(8,128)S(1)}, f32[60,64,128]{2,1,0:T(8,128)S(1)}, f32[60,128]{1,0:T(8,128)S(1)}, f32[60,64,128]{2,1,0:T(8,128)S(1)}) fusion(f32[60,64,128]{2,1,0:T(8,128)S(1)} %get-tuple-element.116, f32[1,64,128]{2,1,0:T(8,128)S(1)} %get-tuple-element.49, f32[59,64,128]{2,1,0:T(8,128)S(1)} %get-tuple-element.51, ...), kind=kLoop, calls=%fused_computation.222 | loop fusion | flops 8832000 | bytes 15851520 | tf_op jit(solution)/shard_map/reduce_sum | solution.py:31
  76.9 2.2 %fusion.58 = (f32[60,64,128]{2,1,0:T(8,128)S(1)}, f32[60,64,128]{2,1,0:T(8,128)S(1)}) fusion(f32[60,64,128]{2,1,0:T(8,128)S(1)} %get-tuple-element.26, f32[60,63,128]{2,1,0:T(8,128)S(1)} %get-tuple-element.37, f32[60,1,128]{2,1,0:T(1,128)S(1)} %get-tuple-element.39, f32[60,1,128]{2,1,0:T(1,128)S(1)} %get-tuple-element.38, ...), kind=kLoop, calls=%fused_computation.95 | loop fusion | flops 7864320 | bytes 15790080 | tf_op jit(solution)/shard_map/sub | solution.py:20
  80.1 2.5 %fusion.106 = (f32[60,128]{1,0:T(8,128)S(1)}, f32[60,64,128]{2,1,0:T(8,128)S(1)}, f32[60,128]{1,0:T(8,128)S(1)}, f32[60,64,128]{2,1,0:T(8,128)S(1)}) fusion(f32[60,64,128]{2,1,0:T(8,128)S(1)} %get-tuple-element.112, f32[1,64,128]{2,1,0:T(8,128)S(1)} %get-tuple-element.33, f32[59,64,128]{2,1,0:T(8,128)S(1)} %get-tuple-element.35, ...), kind=kLoop, calls=%fused_computation.220 | loop fusion | flops 8832000 | bytes 15851520 | tf_op jit(solution)/shard_map/reduce_sum | solution.py:31
  82.6 4.7 %subtract_reduce_fusion.1 = (f32[60,128]{1,0:T(8,128)S(1)}, f32[60,128]{1,0:T(8,128)S(1)}) fusion(bf16[60,64,128]{2,1,0:T(8,128)(2,1)S(1)} %copy-done.2, f32[60,128]{1,0:T(8,128)S(1)} %get-tuple-element.109, f32[60,64,128]{2,1,0:T(8,128)S(1)} %get-tuple-element.111, f32[60,128]{1,0:T(8,128)S(1)} %get-tuple-element.97, ...), kind=kLoop, calls=%fused_computation.106 | loop fusion | flops 18662400 | bytes 17050112 | tf_op jit(solution)/shard_map/reduce_sum | solution.py:82
  87.4 2.1 %subtract_reduce_fusion = (f32[60,128]{1,0:T(8,128)S(1)}, bf16[60,64,128]{2,1,0:T(8,128)(2,1)}) fusion(f32[60,64,128]{2,1,0:T(8,128)S(1)} %get-tuple-element.9, f32[60,128]{1,0:T(8,128)S(1)} %get-tuple-element.96, bf16[60,64,128]{2,1,0:T(8,128)(2,1)S(1)} %copy-done.1, f32[60,128]{1,0:T(8,128)S(1)} %get-tuple-element.104, ...), kind=kLoop, calls=%fused_computation.105 | loop fusion | flops 7365120 | bytes 6021632 | tf_op jit(solution)/shard_map/reduce_sum | solution.py:83
  90.1 3.3 %scatter_custom_fusion.6 = f32[216,1024]{0,1:T(8,128)} fusion(s32[512]{0:T(512)S(1)} %bitcast.125, f32[216,512]{0,1:T(8,128)S(1)} %bitcast_multiply_fusion, f32[]{:T(128)} %constant.100.clone.1), kind=kCustom, calls=%fused_computation.124 | custom fusion | bytes 1409028 | tf_op jit(solution)/shard_map/scatter | solution.py:146
  93.4 9.8 %all-to-all-start.3 = ((f32[216,128,8]{0,2,1:T(8,128)}), f32[216,128,8]{0,2,1:T(8,128)S(1)}, u32[]{:S(2)}, u32[]{:S(2)}) async-start(f32[216,128,8]{0,2,1:T(8,128)} %bitcast.31), calls=%async_computation.3 | async-start | bytes 2097152 | tf_op jit(solution)/shard_map/all_to_all | solution.py:151
  104.6 16.5 %all-to-all-done.3 = f32[216,128,8]{0,2,1:T(8,128)S(1)} async-done(((f32[216,128,8]{0,2,1:T(8,128)}), f32[216,128,8]{0,2,1:T(8,128)S(1)}, u32[]{:S(2)}, u32[]{:S(2)}) %all-to-all-start.3) | async-done | bytes 884768 | tf_op jit(solution)/shard_map/all_to_all | solution.py:151
  121.1 6.2 %scatter_custom_fusion.7 = f32[216,129]{0,1:T(8,128)S(1)} fusion(s32[1024]{0:T(1024)S(1)} %bitcast.122, f32[216,128,8]{0,2,1:T(8,128)S(1)} %all-to-all-done.3, f32[]{:T(128)} %constant.100.clone.1), kind=kCustom, calls=%fused_computation.121 | custom fusion | flops 221184 | bytes 1160036 | tf_op jit(solution)/shard_map/scatter-add | solution.py:157
  (102 shorter events, 23.3 us)
Async XLA Ops:
  0.6 88.9 %copy-start = (f32[72,60]{0,1:T(8,128)S(1)}, f32[72,60]{0,1:T(8,128)}, u32[]{:S(2)}) copy-start(f32[72,60]{0,1:T(8,128)} %param.15) | copy-start | bytes 51844
  0.6 17.9 %copy-start.4 = (s32[4,128]{1,0:T(4,128)S(1)}, s32[4,128]{1,0:T(4,128)}, u32[]{:S(2)}) copy-start(s32[4,128]{1,0:T(4,128)} %param.16) | copy-start | bytes 6148
  0.7 17.9 %copy-start.3 = (bf16[4,72,128]{2,1,0:T(8,128)(2,1)S(1)}, bf16[4,72,128]{2,1,0:T(8,128)(2,1)}, u32[]{:S(2)}) copy-start(bf16[4,72,128]{2,1,0:T(8,128)(2,1)} %param.9) | copy-start | bytes 221188
  5.0 21.3 %all-to-all-start = ((s32[2,128,2]{2,0,1:T(2,128)}), s32[2,128,2]{2,0,1:T(2,128)S(1)}, u32[]{:S(2)}, u32[]{:S(2)}) async-start(s32[2,128,2]{2,0,1:T(2,128)} %copy.32), calls=%async_computation | async-start | bytes 262144 | tf_op jit(solution)/shard_map/all_to_all | solution.py:123
  18.3 31.8 %copy-start.5 = (bf16[60,72]{1,0:T(8,128)(2,1)S(1)}, bf16[60,72]{1,0:T(8,128)(2,1)}, u32[]{:S(2)}) copy-start(bf16[60,72]{1,0:T(8,128)(2,1)} %param.12) | copy-start | bytes 25924
  18.3 32.0 %copy-start.1 = (bf16[60,64,128]{2,1,0:T(8,128)(2,1)S(1)}, bf16[60,64,128]{2,1,0:T(8,128)(2,1)}, u32[]{:S(2)}) copy-start(bf16[60,64,128]{2,1,0:T(8,128)(2,1)} %param.14) | copy-start | bytes 2949124
  18.3 32.0 %copy-start.2 = (bf16[60,64,128]{2,1,0:T(8,128)(2,1)S(1)}, bf16[60,64,128]{2,1,0:T(8,128)(2,1)}, u32[]{:S(2)}) copy-start(bf16[60,64,128]{2,1,0:T(8,128)(2,1)} %param.13) | copy-start | bytes 2949124
  26.3 17.6 %all-to-all-start.1 = ((bf16[288,128,2]{0,2,1:T(2,128)(2,1)}), bf16[288,128,2]{0,2,1:T(2,128)(2,1)S(1)}, u32[]{:S(2)}, u32[]{:S(2)}) async-start(bf16[288,128,2]{0,2,1:T(2,128)(2,1)} %all_to_all.27), calls=%async_computation.1 | async-start | bytes 393216 | tf_op jit(solution)/shard_map/all_to_all | solution.py:122
  43.9 49.5 %all-to-all-start.2 = ((s32[1,128,8]{2,0,1:T(1,128)}), s32[1,128,8]{2,0,1:T(1,128)S(1)}, u32[]{:S(2)}, u32[]{:S(2)}) async-start(s32[1,128,8]{2,0,1:T(1,128)} %bitcast.20), calls=%async_computation.2 | async-start | bytes 131072 | tf_op jit(solution)/shard_map/all_to_all | solution.py:152
  87.4 2.6 %copy-start.6 = (f32[4,128]{1,0:T(4,128)S(1)}, f32[4,128]{1,0:T(4,128)}, u32[]{:S(2)}) copy-start(f32[4,128]{1,0:T(4,128)} %param.17) | copy-start | bytes 6148
  93.4 27.7 %all-to-all-start.3 = ((f32[216,128,8]{0,2,1:T(8,128)}), f32[216,128,8]{0,2,1:T(8,128)S(1)}, u32[]{:S(2)}, u32[]{:S(2)}) async-start(f32[216,128,8]{0,2,1:T(8,128)} %bitcast.31), calls=%async_computation.3 | async-start | bytes 2097152 | tf_op jit(solution)/shard_map/all_to_all | solution.py:151
where the time goes:
time: 128 us
  other arithmetic  40.1 us (31%)
  starting transfers between devices  32.9 us (26%)
  waiting for transfers between devices  27.3 us (21%)
  local copies, waits for them, and re-layouts  25.9 us (20%)
  between operations  1.4 us (1%)
    all_to_all x1, waiting for transfers between devices, body(): lax.all_to_all(values_out, ('sec', 'col'), split_axis=1, concat_axis=1, t...  16.5 us
    all_to_all x1, starting transfers between devices, body(): lax.all_to_all(labels, ('sec', 'col'), split_axis=1, concat_axis=1, tiled...  11.5 us
    reduce_sum x4, other arithmetic, flux_divergence_term(): jnp.mean(field, axis=1, keepdims=True)  10.1 us
    all_to_all x1, starting transfers between devices, body(): lax.all_to_all(values_out, ('sec', 'col'), split_axis=1, concat_axis=1, t...  9.76 us
    sub x4, other arithmetic, flux_divergence_term(): field - jnp.maximum(lateral_stability_factor, 0.0) * (field - left_cells)  9.23 us
    all_to_all x1, waiting for transfers between devices, body(): lax.all_to_all(outgoing, ('sec', 'col'), split_axis=1, concat_axis=1, til...  8.27 us
    all_to_all x1, starting transfers between devices, body(): lax.all_to_all(outgoing, ('sec', 'col'), split_axis=1, concat_axis=1, til...  7.25 us
    scatter-add x1, other arithmetic, body(): node_sum = jnp.zeros((row_count, per_dev + 1), jnp.float32).at[:, got_nod...  6.17 us
  transfers between devices with their start and end apart: 4, of which 3 were waited for; matrix products, arithmetic and copies ran while one was open for 42% of the time, Pallas kernels for 0%

commit v1 on v0

v1 whole, which is shorter than its diff:
```python
import functools
import math

import jax
import jax.numpy as jnp
from jax import lax
from jax.experimental import pallas as pl
from jax.experimental.pallas import tpu as pltpu
from jax.sharding import PartitionSpec as P

LEV = 72
LEVC = 60
CRMX = 64
SUB = 4
COLS = 128
ROWS = 1024
UNROLL = 2
SCALE_T = 0.3 * math.log2(math.e)
SCALE_Q = 1.5 * SCALE_T
LOG_CAPACITY = math.log2(0.5 * SCALE_Q)
MESH = pl.DeviceIdType.MESH
F32 = jnp.float32
BF16 = jnp.bfloat16


def dot_nt(a, b):
    return lax.dot_general(a, b, (((1,), (1,)), ((), ())), preferred_element_type=F32)


def dot_nn(a, b):
    return lax.dot_general(a, b, (((1,), (0,)), ((), ())), preferred_element_type=F32)


def iota(shape, axis):
    return lax.broadcasted_iota(jnp.int32, shape, axis)


def across(row):
    return jnp.broadcast_to(row.astype(F32), (COLS, COLS)).T


def below(x):
    return jnp.where(iota(x.shape, 0) == 0, x, pltpu.roll(x, 1, 0))


def above(x):
    return jnp.where(iota(x.shape, 0) == LEVC - 1, x, pltpu.roll(x, x.shape[0] - 1, 0))


def left(g):
    return jnp.concatenate([pltpu.roll(g[56:64], 1, 0), g[0:56]], axis=0)


def right(g):
    return jnp.concatenate([g[8:64], pltpu.roll(g[0:8], 7, 0)], axis=0)


def split_int(q):
    high = jnp.round(q * (1.0 / 256.0)) * 256.0
    return high.astype(BF16), (q - high).astype(BF16)


def kernel(
    n_sec,
    n_col,
    gcm_ref,
    place_ref,
    switch_ref,
    cmap_ref,
    pt_hbm,
    pm_hbm,
    fmap_ref,
    nid_ref,
    dw_ref,
    crm_hbm,
    node_ref,
    pt,
    pm,
    crm,
    wa,
    qa,
    wb,
    qb,
    ext,
    send_s,
    recv_s,
    pick,
    gain_h,
    gain_l,
    send_n,
    recv_n,
    send_o,
    recv_o,
    cpad,
    fpad,
    c_bx,
    c_cx,
    c_a,
    c_b,
    c_cz,
    c_arg,
    c_neg,
    c_fin,
    c_sum,
    sum_w,
    sum_q,
    in_sem,
    out_sem,
    own_sem,
    tx_sem,
    rx_sem,
):
    n = n_sec * n_col
    rows = ROWS // n
    cap = rows // 4
    my_sec = lax.axis_index("sec")
    my_col = lax.axis_index("col")
    me = my_sec * n_col + my_col

    def peer(step):
        other = lax.rem(me + step, n)
        return other, (other // n_col, lax.rem(other, n_col))

    load_t = pltpu.make_async_copy(pt_hbm, pt, in_sem.at[0])
    load_m = pltpu.make_async_copy(pm_hbm, pm, in_sem.at[1])
    load_t.start()
    load_m.start()

    barrier = pltpu.get_barrier_semaphore()

    def greet(step, carry):
        pl.semaphore_signal(barrier, inc=1, device_id=peer(step)[1], device_id_type=MESH)
        return carry

    lax.fori_loop(1, n, greet, 0)

    def exchange(send, recv, which):
        own = pltpu.make_async_copy(
            send.at[pl.ds(pl.multiple_of(me * rows, rows), rows)],
            recv.at[pl.ds(pl.multiple_of(me * rows, rows), rows)],
            own_sem.at[which],
        )
        own.start()

        def push(step, carry):
            other, device = peer(step)
            pltpu.make_async_remote_copy(
                src_ref=send.at[pl.ds(pl.multiple_of(other * rows, rows), rows)],
                dst_ref=recv.at[pl.ds(pl.multiple_of(me * rows, rows), rows)],
                send_sem=tx_sem.at[which],
                recv_sem=rx_sem.at[which],
                device_id=device,
                device_id_type=MESH,
            ).start()
            return carry

        lax.fori_loop(1, n, push, 0)
        return own

    def all_of(send, recv, which):
        span = pl.ds(0, (n - 1) * rows)
        return pltpu.make_async_remote_copy(
            src_ref=send.at[span],
            dst_ref=recv.at[span],
            send_sem=tx_sem.at[which],
            recv_sem=rx_sem.at[which],
            device_id=peer(1)[1],
            device_id_type=MESH,
        )

    place = place_ref[...]
    dest = place >> 7
    earlier = iota((COLS, COLS), 0) < iota((COLS, COLS), 1)
    dest_f = dest.astype(F32)
    same = (across(dest) == dest_f) & earlier
    rank = jnp.sum(jnp.where(same, 1, 0), axis=0, keepdims=True)
    slot = dest * rows + rank

    label = ((place & 127) + 1).astype(F32)
    flag_in = switch_ref[...].astype(F32)
    at = iota((COLS - LEV, COLS), 0)
    tail = jnp.where(at == 0, label, jnp.where(at == 1, flag_in, 0.0)).astype(BF16)
    for v in range(4):
        ext[0:LEV, v * COLS : (v + 1) * COLS] = gcm_ref[v]
        ext[LEV:COLS, v * COLS : (v + 1) * COLS] = tail

    def pack_state(chunk, carry):
        first = pl.multiple_of(chunk * COLS, COLS)
        row = iota((COLS, COLS), 0) + first
        hot = jnp.concatenate(
            [(row == slot + v * cap).astype(F32).astype(BF16) for v in range(4)], axis=1
        )
        send_s[pl.ds(first, COLS), :] = dot_nt(hot, ext[...]).astype(BF16)
        return carry

    lax.fori_loop(0, ROWS // COLS, pack_state, 0)

    owner = [nid_ref[e : e + 1, :] >> 7 for e in range(4)]
    owner_t = [across(o) for o in owner]
    node_slot = []
    for e in range(4):
        o = owner[e].astype(F32)
        count = jnp.where((owner_t[e] == o) & earlier, 1, 0)
        for other in range(e):
            count = count + jnp.where(owner_t[other] == o, 1, 0)
        node_slot.append(owner[e] * rows + jnp.sum(count, axis=0, keepdims=True))

    def fill_pick(chunk, carry):
        first = pl.multiple_of(chunk * COLS, COLS)
        row = iota((COLS, COLS), 0) + first
        pick[pl.ds(first, COLS), :] = jnp.concatenate(
            [(row == node_slot[e]).astype(F32).astype(BF16) for e in range(4)], axis=1
        )
        return carry

    lax.fori_loop(0, ROWS // COLS, fill_pick, 0)

    cpad[...] = jnp.zeros_like(cpad)
    cpad[0:LEVC, 0:LEV] = cmap_ref[...]
    flag_row = (iota((4, COLS), 0) == 0) & (iota((4, COLS), 1) == LEV + 1)
    cpad[LEVC:64, :] = flag_row.astype(F32).astype(BF16)
    fpad[...] = jnp.zeros_like(fpad)
    fpad[0, :, 0:LEVC] = fmap_ref[...]
    fpad[1, :, 64 : 64 + LEVC] = fmap_ref[...]
    sum_w[...] = jnp.zeros_like(sum_w)
    sum_q[...] = jnp.zeros_like(sum_q)

    pl.semaphore_wait(barrier, n - 1)
    own_s = exchange(send_s, recv_s, 0)

    row_at = iota((CRMX, CRMX), 0)
    regroup = (8 * (row_at % 8) + row_at // 8 == iota((CRMX, CRMX), 1)).astype(F32).astype(BF16)
    load_t.wait()
    load_m.wait()

    def open_row(k, carry):
        both = dot_nn(regroup, jnp.concatenate([pt[k], pm[k]], axis=1))
        w = both[:, 0:COLS] * SCALE_T
        q = both[:, COLS:] * SCALE_Q
        wb[k + 1] = w
        qb[k + 1] = q
        sum_w[pl.ds(k, 1), :] = jnp.sum(w, axis=0, keepdims=True)
        sum_q[pl.ds(k, 1), :] = jnp.sum(q, axis=0, keepdims=True)
        return carry

    lax.fori_loop(0, LEVC, open_row, 0)

    own_s.wait()
    all_of(send_s, recv_s, 0).wait_recv()

    arrived = recv_s[...]
    lane8 = iota((8, COLS), 1)
    labels = dot_nt((lane8 == LEV).astype(F32).astype(BF16), arrived)[0:1, :]
    variable = lax.rem(iota((1, ROWS), 1), rows) // cap
    target = (iota((COLS, 1), 0) + 1).astype(F32)
    profile = []
    for v in range(4):
        mine = jnp.where(variable == v, labels, 0.0)
        hot = (mine == target).astype(F32).astype(BF16)
        placed = dot_nn(hot, arrived).astype(BF16)
        profile.append(dot_nt(cpad[...], placed))
    flag = profile[0][LEVC : LEVC + 1, :]

    cx = 0.45 * jnp.tanh(profile[0])
    cz = 0.3 * jnp.tanh(profile[1])
    keep = 1.0 - jnp.abs(cx)
    az = jnp.abs(cz)
    from_below = cz > 0.0
    c_bx[...] = jnp.abs(cx) / keep
    c_cx[...] = cx
    c_cz[...] = cz
    c_a[...] = (1.0 - az) * keep
    c_b[...] = az * jnp.where(from_below, below(keep), above(keep))

    def lift(x):
        return x - az * (x - jnp.where(from_below, below(x), above(x)))

    goal_w = profile[2] * SCALE_T
    goal_q = profile[3] * SCALE_Q
    start_w = goal_w + sum_w[...] * (1.0 / CRMX)
    start_q = goal_q + sum_q[...] * (1.0 / CRMX)

    goal_n = goal_w + goal_q
    start_n = start_w + start_q
    mean_n = start_n
    for _ in range(SUB):
        lifted = lift(mean_n)
        mean_n = lifted + 0.3 * (goal_n - lifted)

    valid = iota((64, COLS), 0) < LEVC

    def pack_nodes(upper, lower, codes, send):
        upper = jnp.where(valid, upper, 0.0)
        if lower is not None:
            lower = jnp.where(valid, lower, 0.0)
            peak = jnp.maximum(jnp.abs(upper), jnp.abs(lower))
        else:
            peak = jnp.abs(upper)
        peak = jnp.max(peak, axis=0, keepdims=True)
        power = jnp.ceil(jnp.log2(jnp.maximum(peak, 1e-30)))
        unit = jnp.exp2(14.0 - power)
        for e in range(4):
            gain = dw_ref[e : e + 1, :] * unit
            q = jnp.round(upper * gain)
            extra = jnp.where(iota((64, COLS), 0) == LEVC, power, 0.0)
            if codes is not None:
                extra = jnp.where(iota((64, COLS), 0) == LEVC + 1, codes[e], extra)
            high, low = split_int(q + extra)
            gain_h[0:64, e * COLS : (e + 1) * COLS] = high
            gain_l[0:64, e * COLS : (e + 1) * COLS] = low
            if lower is not None:
                high, low = split_int(jnp.round(lower * gain))
                gain_h[64:COLS, e * COLS : (e + 1) * COLS] = high
                gain_l[64:COLS, e * COLS : (e + 1) * COLS] = low
            else:
                gain_h[64:COLS, e * COLS : (e + 1) * COLS] = jnp.zeros((64, COLS), BF16)
                gain_l[64:COLS, e * COLS : (e + 1) * COLS] = jnp.zeros((64, COLS), BF16)

        def push(chunk, carry):
            first = pl.multiple_of(chunk * COLS, COLS)
            hot = pick[pl.ds(first, COLS), :]
            value = dot_nt(hot, gain_h[...]) + dot_nt(hot, gain_l[...])
            send[pl.ds(first, COLS), :] = value.astype(jnp.int32).astype(jnp.int16)
            return carry

        lax.fori_loop(0, ROWS // COLS, push, 0)

    node_code = [((nid_ref[e : e + 1, :] & 127) + 1).astype(F32) for e in range(4)]
    pack_nodes(mean_n - start_n, None, node_code, send_n)
    own_n = exchange(send_n, recv_n, 1)

    def first_x(k, carry):
        here = pl.ds(k, 1)
        bx = c_bx[here, :]
        up = jnp.broadcast_to(c_cx[here, :] > 0.0, (CRMX, COLS))
        for src, dst in ((wb, wa), (qb, qa)):
            g = src[k + 1]
            dst[k + 1] = g + bx * jnp.where(up, left(g), right(g))
        return carry

    lax.fori_loop(0, LEVC, first_x, 0)
    for ref in (wa, qa):
        ref[0] = ref[1]
        ref[LEVC + 1] = ref[LEVC]

    half = 0.5 * flag
    mean_w, mean_q = start_w, start_q
    off_w, off_q = goal_w, goal_q
    cond = jnp.zeros_like(mean_w)
    for sub in range(SUB):
        last = sub == SUB - 1
        source, sink = ((wa, qa), (wb, qb)) if sub % 2 == 0 else ((wb, qb), (wa, qa))
        lifted = lift(mean_w)
        relax = 0.3 * (goal_w - lifted)
        mean_w = lifted + relax
        off_w = lift(off_w) + relax
        lifted = lift(mean_q)
        relax = 0.3 * (goal_q - lifted)
        mean_q = lifted + relax
        off_q = lift(off_q) + relax
        c_arg[...] = off_w + LOG_CAPACITY
        c_neg[...] = -off_q
        off_w = off_w + half * off_q
        if last:
            c_fin[...] = off_w

        def step(it, carry, source=source, sink=sink, last=last):
            k0 = it * UNROLL
            w_rows = [source[0][k0 + u] for u in range(UNROLL + 2)]
            q_rows = [source[1][k0 + u] for u in range(UNROLL + 2)]
            for u in range(UNROLL):
                here = pl.ds(k0 + u, 1)
                a, b = c_a[here, :], c_b[here, :]
                down = jnp.broadcast_to(c_cz[here, :] > 0.0, (CRMX, COLS))
                w = a * w_rows[u + 1] + b * jnp.where(down, w_rows[u], w_rows[u + 2])
                q = a * q_rows[u + 1] + b * jnp.where(down, q_rows[u], q_rows[u + 2])
                gain = jnp.maximum(q - jnp.exp2(w + c_arg[here, :]), c_neg[here, :])
                c_sum[here, :] = jnp.sum(gain, axis=0, keepdims=True)
                gain = half * gain
                w = w + gain
                if last:
                    t = ((w + c_fin[here, :]) * (1.0 / SCALE_T)).astype(BF16)
                    crm[k0 + u] = dot_nn(regroup, t).astype(BF16)
                else:
                    q = q - gain
                    bx = c_bx[here, :]
                    up = jnp.broadcast_to(c_cx[here, :] > 0.0, (CRMX, COLS))
                    sink[0][k0 + u + 1] = w + bx * jnp.where(up, left(w), right(w))
                    sink[1][k0 + u + 1] = q + bx * jnp.where(up, left(q), right(q))
            return carry

        lax.fori_loop(0, LEVC // UNROLL, step, 0)
        if not last:
            for ref in sink:
                ref[0] = ref[1]
                ref[LEVC + 1] = ref[LEVC]
        added = half * (c_sum[...] * (1.0 / CRMX) + off_q)
        off_q = off_q - half * off_q
        mean_w = mean_w + added
        mean_q = mean_q - added
        cond = cond + added

    store = pltpu.make_async_copy(crm, crm_hbm, out_sem.at[0])
    store.start()
    pack_nodes(mean_w - start_w, cond, None, send_o)
    own_o = exchange(send_o, recv_o, 2)

    own_n.wait()
    all_of(send_n, recv_n, 1).wait_recv()

    def gather_rows(recv, code):
        values = recv[...].astype(jnp.int32).astype(F32)
        high, low = split_int(values)
        sel = (lane8 == LEVC + iota((8, COLS), 0)).astype(F32).astype(BF16)
        heads = dot_nt(sel, low) + dot_nt(sel, high)
        unit = jnp.exp2(heads[0:1, :] - 14.0)
        if code is None:
            code = heads[1:2, :]
        hot = jnp.where(code == target, unit, 0.0).astype(BF16)
        total = dot_nn(hot, jnp.concatenate([high, low], axis=1))
        return total[:, 0:COLS] + total[:, COLS:], code

    node_n, code = gather_rows(recv_n, None)
    own_o.wait()
    all_of(send_o, recv_o, 2).wait_recv()
    node_o, _ = gather_rows(recv_o, code)

    def refine(which, x):
        return lax.dot_general(
            fpad[which],
            x,
            (((1,), (1,)), ((), ())),
            precision=lax.Precision.HIGHEST,
            preferred_element_type=F32,
        )

    tend_w = refine(0, node_o)
    tend_c = refine(1, node_o)
    tend_n = refine(0, node_n)
    node_ref[0] = tend_w * (1.0 / SCALE_T)
    node_ref[1] = (tend_n - tend_w) * (1.0 / SCALE_Q)
    node_ref[2] = tend_c * (1.0 / SCALE_Q)

    all_of(send_s, recv_s, 0).wait_send()
    all_of(send_n, recv_n, 1).wait_send()
    all_of(send_o, recv_o, 2).wait_send()
    store.wait()


def solution(mesh):
    n_sec, n_col = mesh.shape["sec"], mesh.shape["col"]

    def body(gcm, place, switch, cmap, pert_temp, pert_moist, fmap, node_ids, weight):
        vmem = pl.BlockSpec(memory_space=pltpu.VMEM)
        hbm = pl.BlockSpec(memory_space=pl.ANY)
        field = pltpu.VMEM((LEVC + 2, CRMX, COLS), F32)
        plane = pltpu.VMEM((64, COLS), F32)
        return pl.pallas_call(
            functools.partial(kernel, n_sec, n_col),
            out_shape=(
                jax.ShapeDtypeStruct((LEVC, CRMX, COLS), BF16),
                jax.ShapeDtypeStruct((3, LEV, COLS), F32),
            ),
            in_specs=[vmem, vmem, vmem, vmem, hbm, hbm, vmem, vmem, vmem],
            out_specs=(hbm, vmem),
            scratch_shapes=[
                pltpu.VMEM((LEVC, CRMX, COLS), BF16),
                pltpu.VMEM((LEVC, CRMX, COLS), BF16),
                pltpu.VMEM((LEVC, CRMX, COLS), BF16),
                field,
                field,
                field,
                field,
                pltpu.VMEM((COLS, 4 * COLS), BF16),
                pltpu.VMEM((ROWS, COLS), BF16),
                pltpu.VMEM((ROWS, COLS), BF16),
                pltpu.VMEM((ROWS, 4 * COLS), BF16),
                pltpu.VMEM((COLS, 4 * COLS), BF16),
                pltpu.VMEM((COLS, 4 * COLS), BF16),
                pltpu.VMEM((ROWS, COLS), jnp.int16),
                pltpu.VMEM((ROWS, COLS), jnp.int16),
                pltpu.VMEM((ROWS, COLS), jnp.int16),
                pltpu.VMEM((ROWS, COLS), jnp.int16),
                pltpu.VMEM((64, COLS), BF16),
                pltpu.VMEM((2, LEV, COLS), F32),
            ]
            + [plane] * 11
            + [
                pltpu.SemaphoreType.DMA((2,)),
                pltpu.SemaphoreType.DMA((1,)),
                pltpu.SemaphoreType.DMA((3,)),
                pltpu.SemaphoreType.DMA((3,)),
                pltpu.SemaphoreType.DMA((3,)),
            ],
            compiler_params=pltpu.CompilerParams(
                collective_id=0, has_side_effects=True, vmem_limit_bytes=48 * 1024 * 1024
            ),
            name="physics_step",
        )(
            gcm,
            place.reshape(1, COLS),
            switch.reshape(1, COLS),
            cmap,
            pert_temp,
            pert_moist,
            fmap,
            node_ids,
            weight,
        )

    block = ("sec", "col")
    return jax.shard_map(
        body,
        mesh=mesh,
        in_specs=(
            P(None, None, block),
            P(block),
            P(block),
            P(),
            P(None, None, block),
            P(None, None, block),
            P(),
            P(None, block),
            P(None, block),
        ),
        out_specs=(P(None, None, block), P(None, None, block)),
        check_vma=False,
    )
```

time: 128 us -> 56.9 us (0.44)
  Pallas kernels: 0 us -> 50.1 us
  other arithmetic: 40.1 us -> 0 us
  starting transfers between devices: 32.9 us -> 0 us
  waiting for transfers between devices: 27.3 us -> 0 us
  local copies, waits for them, and re-layouts: 25.9 us -> 5.76 us
    pallas_call x0 -> x1, Pallas kernels: none -> 50.1 us  [body(): pl.pallas_call(functools.partial(kernel, n_sec, n_col), out_shape=(jax.Sh...]
    all_to_all x4 -> x0, starting transfers between devices: 32.9 us -> none  [the longest x1 11.5 us: body(): lax.all_to_all(labels, ('sec', 'col'), split_axis=1, concat_axis=1, tiled...]
    all_to_all x4 -> x0, waiting for transfers between devices: 27.3 us -> none  [the longest x1 16.5 us: body(): lax.all_to_all(values_out, ('sec', 'col'), split_axis=1, concat_axis=1, t...]
    reduce_sum x8 -> x0, other arithmetic: 17.4 us -> none  [the longest x4 10.1 us: flux_divergence_term(): jnp.mean(field, axis=1, keepdims=True)]
    sub x7 -> x0, other arithmetic: 12.2 us -> none  [the longest x4 9.23 us: flux_divergence_term(): field - jnp.maximum(lateral_stability_factor, 0.0) * (field - left_cells)]
    scatter x7 -> x0, local copies, waits for them, and re-layouts: 11.8 us -> none  [the longest x1 3.29 us: body(): jnp.zeros((row_count, span_node), jnp.float32).at[:, node_slot].set(contrib)]
    slice x37 -> x0, local copies, waits for them, and re-layouts: 10.2 us -> none  [the longest x16 4.91 us: flux_divergence_term(): right_cells = jnp.roll(field, -1, axis=1)]
    scatter-add x1 -> x0, other arithmetic: 6.17 us -> none  [body(): node_sum = jnp.zeros((row_count, per_dev + 1), jnp.float32).at[:, got_nod...]
  transfers between devices with their start and end apart: 4 -> 0, of which waited for: 3 -> 0; matrix products, arithmetic and copies ran while one was open for 42% -> 0% of each run, Pallas kernels for 0% -> 0%
where the time goes in v1:
time: 56.9 us; the launch traced here: 56.6 us
  Pallas kernels  50.1 us (88%)
  local copies, waits for them, and re-layouts  5.76 us (10%)
  between operations  0.73 us (1%)
    pallas_call x1, Pallas kernels, body(): pl.pallas_call(functools.partial(kernel, n_sec, n_col), out_shape=(jax.Sh...  50.1 us
    unnamed x19, local copies, waits for them, and re-layouts  5.76 us

profile of v1, /device:TPU:1, one launch (start us, length us, event | category | flops | bytes accessed | tf_op | source)
XLA Modules:
  0.0 56.6 jit_solution(15578660985590784828)
XLA Ops:
  0.6 0.0 copy-start.3
  0.6 0.0 copy-start.4
  0.7 0.0 copy-start.5
  0.7 0.0 copy-start.6
  0.7 0.0 copy-start.7
  0.7 0.9 %copy.11.fmap_ref = f32[72,60]{1,0:T(8,128)S(1)} copy(f32[72,60]{0,1:T(8,128)} %param.15) | data formatting | bytes 34560 | tf_op args[6]
  1.5 0.0 copy-done.3
  1.6 0.0 copy-done.4
  1.6 0.0 copy-done.5
  1.6 0.0 copy-done.6
  1.6 0.0 copy-done.7
  1.6 0.0 copy-start
  1.6 1.2 %copy-done = bf16[60,64,128]{2,1,0:T(8,128)(2,1)S(1)} copy-done((bf16[60,64,128]{2,1,0:T(8,128)(2,1)S(1)}, bf16[60,64,128]{2,1,0:T(8,128)(2,1)}, u32[]{:S(2)}) %copy-start) | copy-done | bytes 983064
  2.8 0.0 copy-start.1
  2.8 1.2 %copy-done.1 = bf16[60,64,128]{2,1,0:T(8,128)(2,1)S(1)} copy-done((bf16[60,64,128]{2,1,0:T(8,128)(2,1)S(1)}, bf16[60,64,128]{2,1,0:T(8,128)(2,1)}, u32[]{:S(2)}) %copy-start.1) | copy-done | bytes 983064
  4.0 0.0 copy-start.2
  4.0 0.9 %copy-done.2 = bf16[4,72,128]{2,1,0:T(8,128)(2,1)S(1)} copy-done((bf16[4,72,128]{2,1,0:T(8,128)(2,1)S(1)}, bf16[4,72,128]{2,1,0:T(8,128)(2,1)}, u32[]{:S(2)}) %copy-start.2) | copy-done | bytes 73752
  4.9 50.1 %physics_step.1 = (bf16[60,64,128]{2,1,0:T(8,128)(2,1)S(1)}, f32[3,72,128]{2,1,0:T(8,128)S(1)}) custom-call(bf16[4,72,128]{2,1,0:T(8,128)(2,1)S(1)} %copy-done.2, s32[1,128]{1,0:T(1,128)S(1)} %bitcast.2, s32[1,128]{1,0:T(1,128)S(1)} %bitcast.3, bf16[60,72]{1,0:T(8,128)(2,1)S(1)} %copy-done.3, bf16[60,64,128]{2,1,0:T(8,128)(2,1)S(1)} %copy-done, ...), custom_call_target="tpu_custom_call" | custom-call | tf_op jit(solution)/shard_map/physics_step/pallas_call | solution.py:458
  55.0 0.9 %copy.14 = bf16[60,64,128]{2,1,0:T(8,128)(2,1)} copy(bf16[60,64,128]{2,1,0:T(8,128)(2,1)S(1)} %get-tuple-element.4) | data formatting | bytes 1966080
  56.0 0.6 %copy.15 = f32[3,72,128]{2,1,0:T(8,128)} copy(f32[3,72,128]{2,1,0:T(8,128)S(1)} %get-tuple-element.5) | data formatting | bytes 221184
Async XLA Ops:
  0.6 0.9 %copy-start.3 = (bf16[60,72]{1,0:T(8,128)(2,1)S(1)}, bf16[60,72]{1,0:T(8,128)(2,1)}, u32[]{:S(2)}) copy-start(bf16[60,72]{1,0:T(8,128)(2,1)} %cmap_ref.1) | copy-start | bytes 25924
  0.6 0.9 %copy-start.4 = (s32[4,128]{1,0:T(4,128)S(1)}, s32[4,128]{1,0:T(4,128)}, u32[]{:S(2)}) copy-start(s32[4,128]{1,0:T(4,128)} %nid_ref.1) | copy-start | bytes 6148
  0.7 0.9 %copy-start.5 = (f32[4,128]{1,0:T(4,128)S(1)}, f32[4,128]{1,0:T(4,128)}, u32[]{:S(2)}) copy-start(f32[4,128]{1,0:T(4,128)} %dw_ref.1) | copy-start | bytes 6148
  0.7 0.9 %copy-start.6 = (s32[128]{0:T(128)S(1)}, s32[128]{0:T(128)}, u32[]{:S(2)}) copy-start(s32[128]{0:T(128)} %param.10) | copy-start | bytes 1540
  0.7 0.9 %copy-start.7 = (s32[128]{0:T(128)S(1)}, s32[128]{0:T(128)}, u32[]{:S(2)}) copy-start(s32[128]{0:T(128)} %param.11) | copy-start | bytes 1540
  1.6 1.2 %copy-start = (bf16[60,64,128]{2,1,0:T(8,128)(2,1)S(1)}, bf16[60,64,128]{2,1,0:T(8,128)(2,1)}, u32[]{:S(2)}) copy-start(bf16[60,64,128]{2,1,0:T(8,128)(2,1)} %pt_hbm.1) | copy-start | bytes 2949124
  2.8 1.2 %copy-start.1 = (bf16[60,64,128]{2,1,0:T(8,128)(2,1)S(1)}, bf16[60,64,128]{2,1,0:T(8,128)(2,1)}, u32[]{:S(2)}) copy-start(bf16[60,64,128]{2,1,0:T(8,128)(2,1)} %pm_hbm.1) | copy-start | bytes 2949124
  4.0 0.9 %copy-start.2 = (bf16[4,72,128]{2,1,0:T(8,128)(2,1)S(1)}, bf16[4,72,128]{2,1,0:T(8,128)(2,1)}, u32[]{:S(2)}) copy-start(bf16[4,72,128]{2,1,0:T(8,128)(2,1)} %gcm_ref.1) | copy-start | bytes 221188

commit v2 on v1

--- a/solution.py
+++ b/solution.py
@@ -63,16 +63,24 @@
 def kernel(
     n_sec,
     n_col,
+    gcm_hbm,
+    place_hbm,
+    switch_hbm,
+    cmap_hbm,
+    pt_hbm,
+    pm_hbm,
+    fmap_hbm,
+    nid_hbm,
+    dw_hbm,
+    crm_hbm,
+    node_hbm,
     gcm_ref,
     place_ref,
     switch_ref,
     cmap_ref,
-    pt_hbm,
-    pm_hbm,
     fmap_ref,
     nid_ref,
     dw_ref,
-    crm_hbm,
     node_ref,
     pt,
     pm,
@@ -85,8 +93,8 @@
     send_s,
     recv_s,
     pick,
-    gain_h,
-    gain_l,
+    slot_gain,
+    slot_code,
     send_n,
     recv_n,
     send_o,
@@ -117,22 +125,58 @@
     my_col = lax.axis_index("col")
     me = my_sec * n_col + my_col
 
-    def peer(step):
-        other = lax.rem(me + step, n)
-        return other, (other // n_col, lax.rem(other, n_col))
-
-    load_t = pltpu.make_async_copy(pt_hbm, pt, in_sem.at[0])
-    load_m = pltpu.make_async_copy(pm_hbm, pm, in_sem.at[1])
-    load_t.start()
-    load_m.start()
+    my_x, my_z, my_y = my_col // 16, (my_col // 4) % 4, my_col % 4
+
+    def wrap(v):
+        return jnp.where(v >= 4, v - 4, v)
+
+    ys = [wrap(my_y + dy) for dy in (2, 1, 3, 0)]
+    secs = [1 - my_sec, my_sec]
+
+    def each_peer(act):
+        def plane(t, carry):
+            base = wrap(my_x + 1 + wrap(t // 4 + 1)) * 16 + wrap(my_z + 1 + wrap(t % 4 + 1)) * 4
+            for y in ys:
+                col = base + y
+                for sec in secs:
+                    if y is ys[3] and sec is my_sec:
+
+                        @pl.when(t != 10)
+                        def _():
+                            act(sec * n_col + col, (sec, col))
+
+                    else:
+                        act(sec * n_col + col, (sec, col))
+            return carry
+
+        lax.fori_loop(0, 16, plane, 0)
 
     barrier = pltpu.get_barrier_semaphore()
 
-    def greet(step, carry):
-        pl.semaphore_signal(barrier, inc=1, device_id=peer(step)[1], device_id_type=MESH)
-        return carry
-
-    lax.fori_loop(1, n, greet, 0)
+    each_peer(
+        lambda _, device: pl.semaphore_signal(
+            barrier, inc=1, device_id=device, device_id_type=MESH
+        )
+    )
+
+    loads = [
+        pltpu.make_async_copy(src, dst, in_sem.at[i])
+        for i, (src, dst) in enumerate(
+            (
+                (place_hbm, place_ref),
+                (switch_hbm, switch_ref),
+                (gcm_hbm, gcm_ref),
+                (nid_hbm, nid_ref),
+                (dw_hbm, dw_ref),
+                (cmap_hbm, cmap_ref),
+                (fmap_hbm, fmap_ref),
+                (pt_hbm, pt),
+                (pm_hbm, pm),
+            )
+        )
+    ]
+    for load in loads:
+        load.start()
 
     def exchange(send, recv, which):
         own = pltpu.make_async_copy(
@@ -142,8 +186,7 @@
         )
         own.start()
 
-        def push(step, carry):
-            other, device = peer(step)
+        def push(other, device):
             pltpu.make_async_remote_copy(
                 src_ref=send.at[pl.ds(pl.multiple_of(other * rows, rows), rows)],
                 dst_ref=recv.at[pl.ds(pl.multiple_of(me * rows, rows), rows)],
@@ -152,9 +195,8 @@
                 device_id=device,
                 device_id_type=MESH,
             ).start()
-            return carry
-
-        lax.fori_loop(1, n, push, 0)
+
+        each_peer(push)
         return own
 
     def all_of(send, recv, which):
@@ -164,10 +206,12 @@
             dst_ref=recv.at[span],
             send_sem=tx_sem.at[which],
             recv_sem=rx_sem.at[which],
-            device_id=peer(1)[1],
+            device_id=(1 - my_sec, my_col),
             device_id_type=MESH,
         )
 
+    for load in loads[0:3]:
+        load.wait()
     place = place_ref[...]
     dest = place >> 7
     earlier = iota((COLS, COLS), 0) < iota((COLS, COLS), 1)
@@ -195,6 +239,11 @@
 
     lax.fori_loop(0, ROWS // COLS, pack_state, 0)
 
+    pl.semaphore_wait(barrier, n - 1)
+    own_s = exchange(send_s, recv_s, 0)
+
+    for load in loads[3:7]:
+        load.wait()
     owner = [nid_ref[e : e + 1, :] >> 7 for e in range(4)]
     owner_t = [across(o) for o in owner]
     node_slot = []
@@ -205,12 +254,29 @@
             count = count + jnp.where(owner_t[other] == o, 1, 0)
         node_slot.append(owner[e] * rows + jnp.sum(count, axis=0, keepdims=True))
 
+    code = [((nid_ref[e : e + 1, :] & 127) + 1).astype(F32) for e in range(4)]
+    plain = lax.rem(iota((COLS, COLS), 1), 64) >= LEVC
+    to_code = iota((COLS, COLS), 1) == LEVC + 1
+    ones = jnp.ones((COLS, COLS), BF16)
+
     def fill_pick(chunk, carry):
-        first = pl.multiple_of(chunk * COLS, COLS)
-        row = iota((COLS, COLS), 0) + first
-        pick[pl.ds(first, COLS), :] = jnp.concatenate(
-            [(row == node_slot[e]).astype(F32).astype(BF16) for e in range(4)], axis=1
-        )
+        span = pl.ds(pl.multiple_of(chunk * COLS, COLS), COLS)
+        row = iota((COLS, COLS), 0) + chunk * COLS
+        weight = jnp.zeros((COLS, COLS), F32)
+        number = jnp.zeros((COLS, COLS), F32)
+        for e in range(4):
+            hit = row == node_slot[e]
+            weight = jnp.where(hit, dw_ref[e : e + 1, :], weight)
+            number = jnp.where(hit, code[e], number)
+        pick[span, :] = (number > 0.0).astype(F32).astype(BF16)
+        high = weight.astype(BF16)
+        rest = weight - high.astype(F32)
+        mid = rest.astype(BF16)
+        low = (rest - mid.astype(F32)).astype(BF16)
+        weight = dot_nn(high, ones) + (dot_nn(mid, ones) + dot_nn(low, ones))
+        slot_gain[span, :] = jnp.where(plain, 1.0, weight)
+        number = dot_nn(number.astype(BF16), ones)
+        slot_code[span, :] = jnp.where(to_code, number, 0.0)
         return carry
 
     lax.fori_loop(0, ROWS // COLS, fill_pick, 0)
@@ -220,30 +286,31 @@
     flag_row = (iota((4, COLS), 0) == 0) & (iota((4, COLS), 1) == LEV + 1)
     cpad[LEVC:64, :] = flag_row.astype(F32).astype(BF16)
     fpad[...] = jnp.zeros_like(fpad)
-    fpad[0, :, 0:LEVC] = fmap_ref[...]
-    fpad[1, :, 64 : 64 + LEVC] = fmap_ref[...]
+    fpad[0:LEVC, 0:LEV] = fmap_ref[...]
+    fpad[64 : 64 + LEVC, 0:LEV] = fmap_ref[...]
+    fpad[...] = fpad[...].T
     sum_w[...] = jnp.zeros_like(sum_w)
     sum_q[...] = jnp.zeros_like(sum_q)
 
-    pl.semaphore_wait(barrier, n - 1)
-    own_s = exchange(send_s, recv_s, 0)
 
     row_at = iota((CRMX, CRMX), 0)
     regroup = (8 * (row_at % 8) + row_at // 8 == iota((CRMX, CRMX), 1)).astype(F32).astype(BF16)
-    load_t.wait()
-    load_m.wait()
-
-    def open_row(k, carry):
-        both = dot_nn(regroup, jnp.concatenate([pt[k], pm[k]], axis=1))
-        w = both[:, 0:COLS] * SCALE_T
-        q = both[:, COLS:] * SCALE_Q
-        wb[k + 1] = w
-        qb[k + 1] = q
-        sum_w[pl.ds(k, 1), :] = jnp.sum(w, axis=0, keepdims=True)
-        sum_q[pl.ds(k, 1), :] = jnp.sum(q, axis=0, keepdims=True)
+    for load in loads[7:9]:
+        load.wait()
+
+    def open_rows(it, carry):
+        for u in range(4):
+            k = it * 4 + u
+            both = dot_nn(regroup, jnp.concatenate([pt[k], pm[k]], axis=1))
+            w = both[:, 0:COLS] * SCALE_T
+            q = both[:, COLS:] * SCALE_Q
+            wb[k + 1] = w
+            qb[k + 1] = q
+            sum_w[pl.ds(k, 1), :] = jnp.sum(w, axis=0, keepdims=True)
+            sum_q[pl.ds(k, 1), :] = jnp.sum(q, axis=0, keepdims=True)
         return carry
 
-    lax.fori_loop(0, LEVC, open_row, 0)
+    lax.fori_loop(0, LEVC // 4, open_rows, 0)
 
     own_s.wait()
     all_of(send_s, recv_s, 0).wait_recv()
@@ -251,13 +318,13 @@
     arrived = recv_s[...]
     lane8 = iota((8, COLS), 1)
     labels = dot_nt((lane8 == LEV).astype(F32).astype(BF16), arrived)[0:1, :]
-    variable = lax.rem(iota((1, ROWS), 1), rows) // cap
+    variable = (iota((16, COLS), 0) % rows) // cap
     target = (iota((COLS, 1), 0) + 1).astype(F32)
+    hot = (labels == target).astype(F32).astype(BF16)
     profile = []
     for v in range(4):
-        mine = jnp.where(variable == v, labels, 0.0)
-        hot = (mine == target).astype(F32).astype(BF16)
-        placed = dot_nn(hot, arrived).astype(BF16)
+        mine = arrived * jnp.tile((variable == v).astype(F32).astype(BF16), (ROWS // 16, 1))
+        placed = dot_nn(hot, mine).astype(BF16)
         profile.append(dot_nt(cpad[...], placed))
     flag = profile[0][LEVC : LEVC + 1, :]
 
@@ -289,44 +356,32 @@
 
     valid = iota((64, COLS), 0) < LEVC
 
-    def pack_nodes(upper, lower, codes, send):
+    def pack_nodes(upper, lower, send, coded):
         upper = jnp.where(valid, upper, 0.0)
-        if lower is not None:
-            lower = jnp.where(valid, lower, 0.0)
-            peak = jnp.maximum(jnp.abs(upper), jnp.abs(lower))
-        else:
-            peak = jnp.abs(upper)
+        lower = jnp.where(valid, lower, 0.0)
+        peak = jnp.maximum(jnp.abs(upper), jnp.abs(lower))
         peak = jnp.max(peak, axis=0, keepdims=True)
         power = jnp.ceil(jnp.log2(jnp.maximum(peak, 1e-30)))
         unit = jnp.exp2(14.0 - power)
-        for e in range(4):
-            gain = dw_ref[e : e + 1, :] * unit
-            q = jnp.round(upper * gain)
-            extra = jnp.where(iota((64, COLS), 0) == LEVC, power, 0.0)
-            if codes is not None:
-                extra = jnp.where(iota((64, COLS), 0) == LEVC + 1, codes[e], extra)
-            high, low = split_int(q + extra)
-            gain_h[0:64, e * COLS : (e + 1) * COLS] = high
-            gain_l[0:64, e * COLS : (e + 1) * COLS] = low
-            if lower is not None:
-                high, low = split_int(jnp.round(lower * gain))
-                gain_h[64:COLS, e * COLS : (e + 1) * COLS] = high
-                gain_l[64:COLS, e * COLS : (e + 1) * COLS] = low
-            else:
-                gain_h[64:COLS, e * COLS : (e + 1) * COLS] = jnp.zeros((64, COLS), BF16)
-                gain_l[64:COLS, e * COLS : (e + 1) * COLS] = jnp.zeros((64, COLS), BF16)
+        upper = jnp.where(iota((64, COLS), 0) == LEVC, power, upper * unit)
+        value = jnp.concatenate([upper, lower * unit], axis=0).T
+        high = value.astype(BF16)
+        low = (value - high.astype(F32)).astype(BF16)
+        both = jnp.concatenate([high, low], axis=1)
 
         def push(chunk, carry):
-            first = pl.multiple_of(chunk * COLS, COLS)
-            hot = pick[pl.ds(first, COLS), :]
-            value = dot_nt(hot, gain_h[...]) + dot_nt(hot, gain_l[...])
-            send[pl.ds(first, COLS), :] = value.astype(jnp.int32).astype(jnp.int16)
+            span = pl.ds(pl.multiple_of(chunk * 256, 256), 256)
+            out = dot_nn(pick[span, :], both)
+            out = (out[:, 0:COLS] + out[:, COLS:]) * slot_gain[span, :]
+            if coded:
+                out = out + slot_code[span, :]
+            send[span, :] = jnp.round(out).astype(jnp.int32).astype(jnp.int16)
             return carry
 
-        lax.fori_loop(0, ROWS // COLS, push, 0)
-
-    node_code = [((nid_ref[e : e + 1, :] & 127) + 1).astype(F32) for e in range(4)]
-    pack_nodes(mean_n - start_n, None, node_code, send_n)
+        lax.fori_loop(0, ROWS // 256, push, 0)
+
+    change_n = mean_n - start_n
+    pack_nodes(change_n, jnp.zeros_like(change_n), send_n, True)
     own_n = exchange(send_n, recv_n, 1)
 
     def first_x(k, carry):
@@ -379,8 +434,7 @@
                 gain = half * gain
                 w = w + gain
                 if last:
-                    t = ((w + c_fin[here, :]) * (1.0 / SCALE_T)).astype(BF16)
-                    crm[k0 + u] = dot_nn(regroup, t).astype(BF16)
+                    sink[0][k0 + u + 1] = w
                 else:
                     q = q - gain
                     bx = c_bx[here, :]
@@ -400,10 +454,19 @@
         mean_q = mean_q - added
         cond = cond + added
 
+    pack_nodes(mean_w - start_w, cond, send_o, False)
+    own_o = exchange(send_o, recv_o, 2)
+
+    def close_rows(it, carry):
+        for u in range(4):
+            k = it * 4 + u
+            t = ((wa[k + 1] + c_fin[pl.ds(k, 1), :]) * (1.0 / SCALE_T)).astype(BF16)
+            crm[k] = dot_nn(regroup, t).astype(BF16)
+        return carry
+
+    lax.fori_loop(0, LEVC // 4, close_rows, 0)
     store = pltpu.make_async_copy(crm, crm_hbm, out_sem.at[0])
     store.start()
-    pack_nodes(mean_w - start_w, cond, None, send_o)
-    own_o = exchange(send_o, recv_o, 2)
 
     own_n.wait()
     all_of(send_n, recv_n, 1).wait_recv()
@@ -420,14 +483,16 @@
         total = dot_nn(hot, jnp.concatenate([high, low], axis=1))
         return total[:, 0:COLS] + total[:, COLS:], code
 
-    node_n, code = gather_rows(recv_n, None)
+    node_n, codes = gather_rows(recv_n, None)
     own_o.wait()
     all_of(send_o, recv_o, 2).wait_recv()
-    node_o, _ = gather_rows(recv_o, code)
+    node_o, _ = gather_rows(recv_o, codes)
+
+    fine_lane = iota((LEV, COLS), 1) < 64
 
     def refine(which, x):
         return lax.dot_general(
-            fpad[which],
+            jnp.where(fine_lane if which == 0 else ~fine_lane, fpad[0:LEV, :], 0.0),
             x,
             (((1,), (1,)), ((), ())),
             precision=lax.Precision.HIGHEST,
@@ -441,18 +506,20 @@
     node_ref[1] = (tend_n - tend_w) * (1.0 / SCALE_Q)
     node_ref[2] = tend_c * (1.0 / SCALE_Q)
 
+    finish = pltpu.make_async_copy(node_ref, node_hbm, out_sem.at[1])
+    finish.start()
     all_of(send_s, recv_s, 0).wait_send()
     all_of(send_n, recv_n, 1).wait_send()
     all_of(send_o, recv_o, 2).wait_send()
     store.wait()
+    finish.wait()
 
 
 def solution(mesh):
     n_sec, n_col = mesh.shape["sec"], mesh.shape["col"]
 
     def body(gcm, place, switch, cmap, pert_temp, pert_moist, fmap, node_ids, weight):
-        vmem = pl.BlockSpec(memory_space=pltpu.VMEM)
-        hbm = pl.BlockSpec(memory_space=pl.ANY)
+        hbm = pl.BlockSpec(memory_space=pltpu.HBM)
         field = pltpu.VMEM((LEVC + 2, CRMX, COLS), F32)
         plane = pltpu.VMEM((64, COLS), F32)
         return pl.pallas_call(
@@ -461,9 +528,17 @@
                 jax.ShapeDtypeStruct((LEVC, CRMX, COLS), BF16),
                 jax.ShapeDtypeStruct((3, LEV, COLS), F32),
             ),
-            in_specs=[vmem, vmem, vmem, vmem, hbm, hbm, vmem, vmem, vmem],
-            out_specs=(hbm, vmem),
+            in_specs=[hbm] * 9,
+            out_specs=(hbm, hbm),
             scratch_shapes=[
+                pltpu.VMEM((4, LEV, COLS), BF16),
+                pltpu.VMEM((1, COLS), jnp.int32),
+                pltpu.VMEM((1, COLS), jnp.int32),
+                pltpu.VMEM((LEVC, LEV), BF16),
+                pltpu.VMEM((LEVC, LEV), F32),
+                pltpu.VMEM((4, COLS), jnp.int32),
+                pltpu.VMEM((4, COLS), F32),
+                pltpu.VMEM((3, LEV, COLS), F32),
                 pltpu.VMEM((LEVC, CRMX, COLS), BF16),
                 pltpu.VMEM((LEVC, CRMX, COLS), BF16),
                 pltpu.VMEM((LEVC, CRMX, COLS), BF16),
@@ -474,26 +549,26 @@
                 pltpu.VMEM((COLS, 4 * COLS), BF16),
                 pltpu.VMEM((ROWS, COLS), BF16),
                 pltpu.VMEM((ROWS, COLS), BF16),
-                pltpu.VMEM((ROWS, 4 * COLS), BF16),
-                pltpu.VMEM((COLS, 4 * COLS), BF16),
-                pltpu.VMEM((COLS, 4 * COLS), BF16),
+                pltpu.VMEM((ROWS, COLS), BF16),
+                pltpu.VMEM((ROWS, COLS), F32),
+                pltpu.VMEM((ROWS, COLS), F32),
                 pltpu.VMEM((ROWS, COLS), jnp.int16),
                 pltpu.VMEM((ROWS, COLS), jnp.int16),
                 pltpu.VMEM((ROWS, COLS), jnp.int16),
                 pltpu.VMEM((ROWS, COLS), jnp.int16),
                 pltpu.VMEM((64, COLS), BF16),
-                pltpu.VMEM((2, LEV, COLS), F32),
+                pltpu.VMEM((COLS, COLS), F32),
             ]
             + [plane] * 11
             + [
+                pltpu.SemaphoreType.DMA((9,)),
                 pltpu.SemaphoreType.DMA((2,)),
-                pltpu.SemaphoreType.DMA((1,)),
                 pltpu.SemaphoreType.DMA((3,)),
                 pltpu.SemaphoreType.DMA((3,)),
                 pltpu.SemaphoreType.DMA((3,)),
             ],
             compiler_params=pltpu.CompilerParams(
-                collective_id=0, has_side_effects=True, vmem_limit_bytes=48 * 1024 * 1024
+                collective_id=0, has_side_effects=True, vmem_limit_bytes=67043328
             ),
             name="physics_step",
         )(
@@ -503,7 +578,7 @@
             cmap,
             pert_temp,
             pert_moist,
-            fmap,
+            fmap.T,
             node_ids,
             weight,
         )

time: 56.9 us -> 42.8 us (0.75)
  Pallas kernels: 50.1 us -> 39.1 us
  local copies, waits for them, and re-layouts: 5.76 us -> 2.89 us
    pallas_call x1, Pallas kernels: 50.1 us -> 39.1 us  [body(): pl.pallas_call(functools.partial(kernel, n_sec, n_col), out_shape=(jax.Sh...]
    unnamed x19 -> x4, local copies, waits for them, and re-layouts: 5.76 us -> 2.89 us
where the time goes in v2:
time: 42.8 us; the launch traced here: 42.6 us
  Pallas kernels  39.1 us (91%)
  local copies, waits for them, and re-layouts  2.89 us (7%)
  between operations  0.65 us (2%)
    pallas_call x1, Pallas kernels, body(): pl.pallas_call(functools.partial(kernel, n_sec, n_col), out_shape=(jax.Sh...  39.1 us
    unnamed x4, local copies, waits for them, and re-layouts  2.89 us

profile of v2, /device:TPU:1, one launch (start us, length us, event | category | flops | bytes accessed | tf_op | source)
XLA Modules:
  0.0 42.6 jit_solution(8787493786634640388)
XLA Ops:
  0.6 39.1 %physics_step.1 = (bf16[60,64,128]{2,1,0:T(8,128)(2,1)}, f32[3,72,128]{2,1,0:T(8,128)}) custom-call(bf16[4,72,128]{2,1,0:T(8,128)(2,1)} %gcm_hbm.1, s32[1,128]{1,0:T(1,128)} %bitcast.4, s32[1,128]{1,0:T(1,128)} %bitcast.5, bf16[60,72]{1,0:T(8,128)(2,1)} %cmap_hbm.1, bf16[60,64,128]{2,1,0:T(8,128)(2,1)} %pt_hbm.1, bf16[60,64,128]{2,1,0:T(8,128)(2,1)} %pm_hbm.1, ...), custom_call_target="tpu_custom_call" | custom-call | tf_op jit(solution)/shard_map/physics_step/pallas_call | solution.py:525
  39.7 0.0 copy-start
  39.7 2.2 %copy.13 = bf16[60,64,128]{2,1,0:T(8,128)(2,1)} copy(bf16[60,64,128]{2,1,0:T(8,128)(2,1)} %get-tuple-element.4) | data formatting | bytes 1966080
  42.0 0.0 copy-done
  42.0 0.6 %copy.14 = f32[3,72,128]{2,1,0:T(8,128)} copy(f32[3,72,128]{2,1,0:T(8,128)S(1)} %copy-done) | data formatting | bytes 221184
Async XLA Ops:
  39.7 2.3 %copy-start = (f32[3,72,128]{2,1,0:T(8,128)S(1)}, f32[3,72,128]{2,1,0:T(8,128)}, u32[]{:S(2)}) copy-start(f32[3,72,128]{2,1,0:T(8,128)} %get-tuple-element.5) | copy-start | bytes 331780

commit v3 on v2

--- a/solution.py
+++ b/solution.py
@@ -72,8 +72,11 @@
     fmap_hbm,
     nid_hbm,
     dw_hbm,
-    crm_hbm,
-    node_hbm,
+    crm,
+    recv_o,
+    codes_ref,
+    tend_ref,
+    fine_ref,
     gcm_ref,
     place_ref,
     switch_ref,
@@ -81,10 +84,8 @@
     fmap_ref,
     nid_ref,
     dw_ref,
-    node_ref,
     pt,
     pm,
-    crm,
     wa,
     qa,
     wb,
@@ -98,7 +99,6 @@
     send_n,
     recv_n,
     send_o,
-    recv_o,
     cpad,
     fpad,
     c_bx,
@@ -113,7 +113,6 @@
     sum_w,
     sum_q,
     in_sem,
-    out_sem,
     own_sem,
     tx_sem,
     rx_sem,
@@ -288,7 +287,6 @@
     fpad[...] = jnp.zeros_like(fpad)
     fpad[0:LEVC, 0:LEV] = fmap_ref[...]
     fpad[64 : 64 + LEVC, 0:LEV] = fmap_ref[...]
-    fpad[...] = fpad[...].T
     sum_w[...] = jnp.zeros_like(sum_w)
     sum_q[...] = jnp.zeros_like(sum_q)
 
@@ -465,54 +463,59 @@
         return carry
 
     lax.fori_loop(0, LEVC // 4, close_rows, 0)
-    store = pltpu.make_async_copy(crm, crm_hbm, out_sem.at[0])
-    store.start()
-
     own_n.wait()
     all_of(send_n, recv_n, 1).wait_recv()
 
-    def gather_rows(recv, code):
-        values = recv[...].astype(jnp.int32).astype(F32)
-        high, low = split_int(values)
-        sel = (lane8 == LEVC + iota((8, COLS), 0)).astype(F32).astype(BF16)
-        heads = dot_nt(sel, low) + dot_nt(sel, high)
-        unit = jnp.exp2(heads[0:1, :] - 14.0)
-        if code is None:
-            code = heads[1:2, :]
-        hot = jnp.where(code == target, unit, 0.0).astype(BF16)
-        total = dot_nn(hot, jnp.concatenate([high, low], axis=1))
-        return total[:, 0:COLS] + total[:, COLS:], code
-
-    node_n, codes = gather_rows(recv_n, None)
-    own_o.wait()
-    all_of(send_o, recv_o, 2).wait_recv()
-    node_o, _ = gather_rows(recv_o, codes)
-
-    fine_lane = iota((LEV, COLS), 1) < 64
-
-    def refine(which, x):
-        return lax.dot_general(
-            jnp.where(fine_lane if which == 0 else ~fine_lane, fpad[0:LEV, :], 0.0),
-            x,
-            (((1,), (1,)), ((), ())),
-            precision=lax.Precision.HIGHEST,
-            preferred_element_type=F32,
-        )
-
-    tend_w = refine(0, node_o)
-    tend_c = refine(1, node_o)
-    tend_n = refine(0, node_n)
-    node_ref[0] = tend_w * (1.0 / SCALE_T)
-    node_ref[1] = (tend_n - tend_w) * (1.0 / SCALE_Q)
-    node_ref[2] = tend_c * (1.0 / SCALE_Q)
-
-    finish = pltpu.make_async_copy(node_ref, node_hbm, out_sem.at[1])
-    finish.start()
+    values_n = spread(recv_n)
+    sel = (lane8 == LEVC + iota((8, COLS), 0)).astype(F32).astype(BF16)
+    codes_ref[...] = dot_nt(sel, values_n[1])
+    node_n = sum_rows(values_n, codes_ref[...], codes_ref[...])
+    fine_ref[...] = fpad[...].T
+    tend_ref[...] = refine(fine_ref, 0, node_n)
     all_of(send_s, recv_s, 0).wait_send()
     all_of(send_n, recv_n, 1).wait_send()
-    all_of(send_o, recv_o, 2).wait_send()
+    own_o.wait()
+    all_of(send_o, recv_o, 2).wait()
+
+
+def spread(recv):
+    return split_int(recv[...].astype(jnp.int32).astype(F32))
+
+
+def sum_rows(values, power, code):
+    unit = jnp.exp2(power[0:1, :] - 14.0)
+    target = (iota((COLS, 1), 0) + 1).astype(F32)
+    hot = jnp.where(code[1:2, :] == target, unit, 0.0).astype(BF16)
+    total = dot_nn(hot, jnp.concatenate(values, axis=1))
+    return total[:, 0:COLS] + total[:, COLS:]
+
+
+def refine(fine_ref, which, x):
+    fine_lane = iota((LEV, COLS), 1) < 64
+    return lax.dot_general(
+        jnp.where(fine_lane if which == 0 else ~fine_lane, fine_ref[0:LEV, :], 0.0),
+        x,
+        (((1,), (1,)), ((), ())),
+        precision=lax.Precision.HIGHEST,
+        preferred_element_type=F32,
+    )
+
+
+def finish(crm, recv_o, codes_ref, tend_ref, fine_ref, crm_out, node_out, node, sem):
+    store = pltpu.make_async_copy(crm, crm_out, sem.at[0])
+    store.start()
+    values = spread(recv_o)
+    sel = (iota((8, COLS), 1) == LEVC).astype(F32).astype(BF16)
+    power = dot_nt(sel, values[1])
+    node_o = sum_rows(values, power, codes_ref[...])
+    tend_w = refine(fine_ref, 0, node_o)
+    node[0] = tend_w * (1.0 / SCALE_T)
+    node[1] = (tend_ref[...] - tend_w) * (1.0 / SCALE_Q)
+    node[2] = refine(fine_ref, 1, node_o) * (1.0 / SCALE_Q)
+    close = pltpu.make_async_copy(node, node_out, sem.at[1])
+    close.start()
     store.wait()
-    finish.wait()
+    close.wait()
 
 
 def solution(mesh):
@@ -522,14 +525,18 @@
         hbm = pl.BlockSpec(memory_space=pltpu.HBM)
         field = pltpu.VMEM((LEVC + 2, CRMX, COLS), F32)
         plane = pltpu.VMEM((64, COLS), F32)
-        return pl.pallas_call(
+        vmem = pl.BlockSpec(memory_space=pltpu.VMEM)
+        between = pl.pallas_call(
             functools.partial(kernel, n_sec, n_col),
             out_shape=(
-                jax.ShapeDtypeStruct((LEVC, CRMX, COLS), BF16),
-                jax.ShapeDtypeStruct((3, LEV, COLS), F32),
+                pltpu.VMEM((LEVC, CRMX, COLS), BF16),
+                pltpu.VMEM((ROWS, COLS), jnp.int16),
+                pltpu.VMEM((8, ROWS), F32),
+                pltpu.VMEM((LEV, COLS), F32),
+                pltpu.VMEM((COLS, COLS), F32),
             ),
             in_specs=[hbm] * 9,
-            out_specs=(hbm, hbm),
+            out_specs=(vmem,) * 5,
             scratch_shapes=[
                 pltpu.VMEM((4, LEV, COLS), BF16),
                 pltpu.VMEM((1, COLS), jnp.int32),
@@ -538,8 +545,6 @@
                 pltpu.VMEM((LEVC, LEV), F32),
                 pltpu.VMEM((4, COLS), jnp.int32),
                 pltpu.VMEM((4, COLS), F32),
-                pltpu.VMEM((3, LEV, COLS), F32),
-                pltpu.VMEM((LEVC, CRMX, COLS), BF16),
                 pltpu.VMEM((LEVC, CRMX, COLS), BF16),
                 pltpu.VMEM((LEVC, CRMX, COLS), BF16),
                 field,
@@ -555,20 +560,18 @@
                 pltpu.VMEM((ROWS, COLS), jnp.int16),
                 pltpu.VMEM((ROWS, COLS), jnp.int16),
                 pltpu.VMEM((ROWS, COLS), jnp.int16),
-                pltpu.VMEM((ROWS, COLS), jnp.int16),
                 pltpu.VMEM((64, COLS), BF16),
                 pltpu.VMEM((COLS, COLS), F32),
             ]
             + [plane] * 11
             + [
                 pltpu.SemaphoreType.DMA((9,)),
-                pltpu.SemaphoreType.DMA((2,)),
                 pltpu.SemaphoreType.DMA((3,)),
                 pltpu.SemaphoreType.DMA((3,)),
                 pltpu.SemaphoreType.DMA((3,)),
             ],
             compiler_params=pltpu.CompilerParams(
-                collective_id=0, has_side_effects=True, vmem_limit_bytes=67043328
+                collective_id=0, has_side_effects=True, vmem_limit_bytes=65000000
             ),
             name="physics_step",
         )(
@@ -582,6 +585,21 @@
             node_ids,
             weight,
         )
+        return pl.pallas_call(
+            finish,
+            out_shape=(
+                jax.ShapeDtypeStruct((LEVC, CRMX, COLS), BF16),
+                jax.ShapeDtypeStruct((3, LEV, COLS), F32),
+            ),
+            in_specs=[vmem] * 5,
+            out_specs=(hbm, hbm),
+            scratch_shapes=[
+                pltpu.VMEM((3, LEV, COLS), F32),
+                pltpu.SemaphoreType.DMA((2,)),
+            ],
+            compiler_params=pltpu.CompilerParams(vmem_limit_bytes=8 * 1024 * 1024),
+            name="sum_on_nodes",
+        )(*between)
 
     block = ("sec", "col")
     return jax.shard_map(

time: 42.8 us -> 39.5 us (0.923)
  local copies, waits for them, and re-layouts: 2.89 us -> 0 us
    unnamed x4 -> x0, local copies, waits for them, and re-layouts: 2.89 us -> none
    pallas_call x1 -> x2, Pallas kernels: 39.1 us -> 38.8 us  [the longest x1 37.3 us: body(): pl.pallas_call(functools.partial(kernel, n_sec, n_col), out_shape=(pltpu....]
where the time goes in v3:
time: 39.5 us; the launch traced here: 39.4 us
  Pallas kernels  38.8 us (98%)
  between operations  0.64 us (2%)
    pallas_call x1, Pallas kernels, body(): pl.pallas_call(functools.partial(kernel, n_sec, n_col), out_shape=(pltpu....  37.3 us
    pallas_call x1, Pallas kernels, body(): pl.pallas_call(finish, out_shape=(jax.ShapeDtypeStruct((LEVC, CRMX, COLS)...  1.45 us

profile of v3, /device:TPU:1, one launch (start us, length us, event | category | flops | bytes accessed | tf_op | source)
XLA Modules:
  0.0 39.4 jit_solution(10246373716173059574)
XLA Ops:
  0.6 37.3 %physics_step.1 = (bf16[60,64,128]{2,1,0:T(8,128)(2,1)S(1)}, s16[1024,128]{1,0:T(8,128)(2,1)S(1)}, f32[8,1024]{1,0:T(8,128)S(1)}, f32[72,128]{1,0:T(8,128)S(1)}, f32[128,128]{1,0:T(8,128)S(1)}) custom-call(bf16[4,72,128]{2,1,0:T(8,128)(2,1)} %gcm_hbm.1, s32[1,128]{1,0:T(1,128)} %bitcast.4, s32[1,128]{1,0:T(1,128)} %bitcast.5, bf16[60,72]{1,0:T(8,128)(2,1)} %cmap_hbm.1, ...), custom_call_target="tpu_custom_call" | custom-call | tf_op jit(solution)/shard_map/physics_step/pallas_call | solution.py:529
  38.0 1.4 %sum_on_nodes.1 = (bf16[60,64,128]{2,1,0:T(8,128)(2,1)}, f32[3,72,128]{2,1,0:T(8,128)}) custom-call(bf16[60,64,128]{2,1,0:T(8,128)(2,1)S(1)} %get-tuple-element.7.crm, s16[1024,128]{1,0:T(8,128)(2,1)S(1)} %get-tuple-element.8.recv_o, f32[8,1024]{1,0:T(8,128)S(1)} %get-tuple-element.9.codes_ref, f32[72,128]{1,0:T(8,128)S(1)} %get-tuple-element.10.tend_ref, ...), custom_call_target="tpu_custom_call" | custom-call | tf_op jit(solution)/shard_map/sum_on_nodes/pallas_call | solution.py:588

commit v4 on v3

--- a/solution.py
+++ b/solution.py
@@ -14,7 +14,10 @@
 SUB = 4
 COLS = 128
 ROWS = 1024
-UNROLL = 2
+TAIL = 4 * LEV - 2 * COLS
+PIECES = 3
+UNROLL = 4
+STEPS = LEVC // UNROLL
 SCALE_T = 0.3 * math.log2(math.e)
 SCALE_Q = 1.5 * SCALE_T
 LOG_CAPACITY = math.log2(0.5 * SCALE_Q)
@@ -40,11 +43,11 @@
 
 
 def below(x):
-    return jnp.where(iota(x.shape, 0) == 0, x, pltpu.roll(x, 1, 0))
+    return pltpu.roll(x, 1, 0)
 
 
 def above(x):
-    return jnp.where(iota(x.shape, 0) == LEVC - 1, x, pltpu.roll(x, x.shape[0] - 1, 0))
+    return pltpu.roll(x, x.shape[0] - 1, 0)
 
 
 def left(g):
@@ -99,6 +102,7 @@
     send_n,
     recv_n,
     send_o,
+    halves,
     cpad,
     fpad,
     c_bx,
@@ -119,7 +123,9 @@
 ):
     n = n_sec * n_col
     rows = ROWS // n
-    cap = rows // 4
+    cap = 2 * COLS // n
+    span_s = n * PIECES * cap
+    send_rows, recv_rows = send_s.reshape(span_s, COLS), recv_s.reshape(span_s, COLS)
     my_sec = lax.axis_index("sec")
     my_col = lax.axis_index("col")
     me = my_sec * n_col + my_col
@@ -133,8 +139,10 @@
     secs = [1 - my_sec, my_sec]
 
     def each_peer(act):
-        def plane(t, carry):
-            base = wrap(my_x + 1 + wrap(t // 4 + 1)) * 16 + wrap(my_z + 1 + wrap(t % 4 + 1)) * 4
+        def plane(t):
+            x = wrap(wrap(my_x + 2 + lax.div(t, 4)))
+            z = wrap(wrap(my_z + 2 + lax.rem(t, 4)))
+            base = x * 16 + z * 4
             for y in ys:
                 col = base + y
                 for sec in secs:
@@ -146,17 +154,15 @@
 
                     else:
                         act(sec * n_col + col, (sec, col))
+
+        return plane
+
+    def repeat(body, low, high):
+        def step(i, carry):
+            body(i)
             return carry
 
-        lax.fori_loop(0, 16, plane, 0)
-
-    barrier = pltpu.get_barrier_semaphore()
-
-    each_peer(
-        lambda _, device: pl.semaphore_signal(
-            barrier, inc=1, device_id=device, device_id_type=MESH
-        )
-    )
+        lax.fori_loop(low, high, step, 0)
 
     loads = [
         pltpu.make_async_copy(src, dst, in_sem.at[i])
@@ -174,32 +180,45 @@
             )
         )
     ]
-    for load in loads:
+    for load in loads[0:3]:
         load.start()
 
+    barrier = pltpu.get_barrier_semaphore()
+
+    greet = each_peer(
+        lambda _, device: pl.semaphore_signal(
+            barrier, inc=1, device_id=device, device_id_type=MESH
+        )
+    )
+    repeat(greet, 0, 16)
+    for load in loads[3:]:
+        load.start()
+
     def exchange(send, recv, which):
+        unit = send.shape[0] // n
+
+        def block(device):
+            return pl.ds(device * unit, unit)
+
         own = pltpu.make_async_copy(
-            send.at[pl.ds(pl.multiple_of(me * rows, rows), rows)],
-            recv.at[pl.ds(pl.multiple_of(me * rows, rows), rows)],
-            own_sem.at[which],
+            send.at[block(me)], recv.at[block(me)], own_sem.at[which]
         )
         own.start()
 
         def push(other, device):
             pltpu.make_async_remote_copy(
-                src_ref=send.at[pl.ds(pl.multiple_of(other * rows, rows), rows)],
-                dst_ref=recv.at[pl.ds(pl.multiple_of(me * rows, rows), rows)],
+                src_ref=send.at[block(other)],
+                dst_ref=recv.at[block(me)],
                 send_sem=tx_sem.at[which],
                 recv_sem=rx_sem.at[which],
                 device_id=device,
                 device_id_type=MESH,
             ).start()
 
-        each_peer(push)
-        return own
+        return own, each_peer(push)
 
     def all_of(send, recv, which):
-        span = pl.ds(0, (n - 1) * rows)
+        span = pl.ds(0, send.shape[0] // n * (n - 1))
         return pltpu.make_async_remote_copy(
             src_ref=send.at[span],
             dst_ref=recv.at[span],
@@ -217,29 +236,37 @@
     dest_f = dest.astype(F32)
     same = (across(dest) == dest_f) & earlier
     rank = jnp.sum(jnp.where(same, 1, 0), axis=0, keepdims=True)
-    slot = dest * rows + rank
+    slot = dest * (PIECES * cap) + rank
 
     label = ((place & 127) + 1).astype(F32)
     flag_in = switch_ref[...].astype(F32)
-    at = iota((COLS - LEV, COLS), 0)
-    tail = jnp.where(at == 0, label, jnp.where(at == 1, flag_in, 0.0)).astype(BF16)
     for v in range(4):
-        ext[0:LEV, v * COLS : (v + 1) * COLS] = gcm_ref[v]
-        ext[LEV:COLS, v * COLS : (v + 1) * COLS] = tail
-
-    def pack_state(chunk, carry):
-        first = pl.multiple_of(chunk * COLS, COLS)
-        row = iota((COLS, COLS), 0) + first
+        first = v * LEV
+        while first < (v + 1) * LEV:
+            piece, at = first // COLS, first % COLS
+            size = min(COLS - at, (v + 1) * LEV - first)
+            ext[at : at + size, piece * COLS : (piece + 1) * COLS] = gcm_ref[
+                v, first - v * LEV : first - v * LEV + size, :
+            ]
+            first += size
+    at = iota((COLS - TAIL, COLS), 0)
+    tail = jnp.where(at == 0, label, jnp.where(at == 1, flag_in, 0.0))
+    ext[TAIL:COLS, 2 * COLS : 3 * COLS] = tail.astype(BF16)
+
+    def pack_state(chunk):
+        row = iota((COLS, COLS), 0) + chunk * COLS
         hot = jnp.concatenate(
-            [(row == slot + v * cap).astype(F32).astype(BF16) for v in range(4)], axis=1
+            [(row == slot + f * cap).astype(F32).astype(BF16) for f in range(PIECES)], axis=1
         )
-        send_s[pl.ds(first, COLS), :] = dot_nt(hot, ext[...]).astype(BF16)
-        return carry
-
-    lax.fori_loop(0, ROWS // COLS, pack_state, 0)
+        send_rows[pl.ds(pl.multiple_of(chunk * COLS, COLS), COLS), :] = dot_nt(
+            hot, ext[...]
+        ).astype(BF16)
+
+    repeat(pack_state, 0, span_s // COLS)
 
     pl.semaphore_wait(barrier, n - 1)
-    own_s = exchange(send_s, recv_s, 0)
+    own_s, push_s = exchange(send_s, recv_s, 0)
+    repeat(push_s, 0, 16)
 
     for load in loads[3:7]:
         load.wait()
@@ -281,12 +308,16 @@
     lax.fori_loop(0, ROWS // COLS, fill_pick, 0)
 
     cpad[...] = jnp.zeros_like(cpad)
-    cpad[0:LEVC, 0:LEV] = cmap_ref[...]
-    flag_row = (iota((4, COLS), 0) == 0) & (iota((4, COLS), 1) == LEV + 1)
-    cpad[LEVC:64, :] = flag_row.astype(F32).astype(BF16)
+    for v in range(4):
+        cpad[v * 64 : v * 64 + LEVC, v * LEV : (v + 1) * LEV] = cmap_ref[...]
+    flag_row = (iota((4, COLS), 0) == 0) & (iota((4, COLS), 1) == TAIL + 1)
+    cpad[LEVC:64, 2 * COLS : 3 * COLS] = flag_row.astype(F32).astype(BF16)
     fpad[...] = jnp.zeros_like(fpad)
     fpad[0:LEVC, 0:LEV] = fmap_ref[...]
     fpad[64 : 64 + LEVC, 0:LEV] = fmap_ref[...]
+    for ref in (wa, qa, wb, qb):
+        ref[0] = jnp.zeros((CRMX, COLS), F32)
+        ref[LEVC + 1] = jnp.zeros((CRMX, COLS), F32)
     sum_w[...] = jnp.zeros_like(sum_w)
     sum_q[...] = jnp.zeros_like(sum_q)
 
@@ -313,24 +344,33 @@
     own_s.wait()
     all_of(send_s, recv_s, 0).wait_recv()
 
-    arrived = recv_s[...]
+    arrived = recv_rows[...]
     lane8 = iota((8, COLS), 1)
-    labels = dot_nt((lane8 == LEV).astype(F32).astype(BF16), arrived)[0:1, :]
-    variable = (iota((16, COLS), 0) % rows) // cap
+    labels = dot_nt((lane8 == TAIL).astype(F32).astype(BF16), arrived)[0:1, :]
+    piece = lax.rem(iota((1, span_s), 1), PIECES * cap) // cap
+    labels = jnp.where(piece == 2, labels, 0.0)
+    labels = labels + (
+        pltpu.roll(labels, span_s - cap, 1) + pltpu.roll(labels, span_s - 2 * cap, 1)
+    )
     target = (iota((COLS, 1), 0) + 1).astype(F32)
     hot = (labels == target).astype(F32).astype(BF16)
-    profile = []
-    for v in range(4):
-        mine = arrived * jnp.tile((variable == v).astype(F32).astype(BF16), (ROWS // 16, 1))
-        placed = dot_nn(hot, mine).astype(BF16)
-        profile.append(dot_nt(cpad[...], placed))
+    period = PIECES * 16
+    piece = lax.rem(iota((period, COLS), 0), PIECES * cap) // cap
+    placed = []
+    for f in range(PIECES):
+        mine = jnp.tile((piece == f).astype(F32).astype(BF16), (span_s // period, 1)) * arrived
+        placed.append(dot_nn(hot, mine).astype(BF16))
+    profiles = dot_nt(cpad[...], jnp.concatenate(placed, axis=1))
+    profile = [profiles[v * 64 : (v + 1) * 64] for v in range(4)]
     flag = profile[0][LEVC : LEVC + 1, :]
 
     cx = 0.45 * jnp.tanh(profile[0])
     cz = 0.3 * jnp.tanh(profile[1])
     keep = 1.0 - jnp.abs(cx)
-    az = jnp.abs(cz)
     from_below = cz > 0.0
+    level = iota((64, COLS), 0)
+    outside = (from_below & (level == 0)) | (~from_below & (level == LEVC - 1))
+    az = jnp.where(outside, 0.0, jnp.abs(cz))
     c_bx[...] = jnp.abs(cx) / keep
     c_cx[...] = cx
     c_cz[...] = cz
@@ -365,22 +405,21 @@
         value = jnp.concatenate([upper, lower * unit], axis=0).T
         high = value.astype(BF16)
         low = (value - high.astype(F32)).astype(BF16)
-        both = jnp.concatenate([high, low], axis=1)
-
-        def push(chunk, carry):
-            span = pl.ds(pl.multiple_of(chunk * 256, 256), 256)
-            out = dot_nn(pick[span, :], both)
+        halves[...] = jnp.concatenate([high, low], axis=1)
+
+        def pack(chunk, size):
+            span = pl.ds(pl.multiple_of(chunk * size, size), size)
+            out = dot_nn(pick[span, :], halves[...])
             out = (out[:, 0:COLS] + out[:, COLS:]) * slot_gain[span, :]
             if coded:
                 out = out + slot_code[span, :]
-            send[span, :] = jnp.round(out).astype(jnp.int32).astype(jnp.int16)
-            return carry
-
-        lax.fori_loop(0, ROWS // 256, push, 0)
+            send.reshape(ROWS, COLS)[span, :] = jnp.round(out).astype(jnp.int32).astype(jnp.int16)
+
+        return pack
 
     change_n = mean_n - start_n
-    pack_nodes(change_n, jnp.zeros_like(change_n), send_n, True)
-    own_n = exchange(send_n, recv_n, 1)
+    pack_n = pack_nodes(change_n, jnp.zeros_like(change_n), send_n, True)
+    pack_n(STEPS, 64)
 
     def first_x(k, carry):
         here = pl.ds(k, 1)
@@ -392,9 +431,6 @@
         return carry
 
     lax.fori_loop(0, LEVC, first_x, 0)
-    for ref in (wa, qa):
-        ref[0] = ref[1]
-        ref[LEVC + 1] = ref[LEVC]
 
     half = 0.5 * flag
     mean_w, mean_q = start_w, start_q
@@ -417,8 +453,12 @@
         if last:
             c_fin[...] = off_w
 
-        def step(it, carry, source=source, sink=sink, last=last):
+        def step(it, carry, source=source, sink=sink, last=last, sub=sub):
             k0 = it * UNROLL
+            if sub == 0:
+                pack_n(it, 64)
+            if sub == 1:
+                push_n(it)
             w_rows = [source[0][k0 + u] for u in range(UNROLL + 2)]
             q_rows = [source[1][k0 + u] for u in range(UNROLL + 2)]
             for u in range(UNROLL):
@@ -441,19 +481,20 @@
                     sink[1][k0 + u + 1] = q + bx * jnp.where(up, left(q), right(q))
             return carry
 
-        lax.fori_loop(0, LEVC // UNROLL, step, 0)
-        if not last:
-            for ref in sink:
-                ref[0] = ref[1]
-                ref[LEVC + 1] = ref[LEVC]
+        if sub == 1:
+            own_n, push_n = exchange(send_n, recv_n, 1)
+            push_n(STEPS)
+        lax.fori_loop(0, STEPS, step, 0)
         added = half * (c_sum[...] * (1.0 / CRMX) + off_q)
         off_q = off_q - half * off_q
         mean_w = mean_w + added
         mean_q = mean_q - added
         cond = cond + added
 
-    pack_nodes(mean_w - start_w, cond, send_o, False)
-    own_o = exchange(send_o, recv_o, 2)
+    pack_o = pack_nodes(mean_w - start_w, cond, send_o, False)
+    repeat(lambda i: pack_o(i, 256), 0, ROWS // 256)
+    own_o, push_o = exchange(send_o, recv_o, 2)
+    repeat(push_o, 0, 16)
 
     def close_rows(it, carry):
         for u in range(4):
@@ -479,7 +520,7 @@
 
 
 def spread(recv):
-    return split_int(recv[...].astype(jnp.int32).astype(F32))
+    return split_int(recv.reshape(ROWS, COLS)[...].astype(jnp.int32).astype(F32))
 
 
 def sum_rows(values, power, code):
@@ -502,8 +543,12 @@
 
 
 def finish(crm, recv_o, codes_ref, tend_ref, fine_ref, crm_out, node_out, node, sem):
-    store = pltpu.make_async_copy(crm, crm_out, sem.at[0])
-    store.start()
+    stores = [
+        pltpu.make_async_copy(crm.at[pl.ds(i * 15, 15)], crm_out.at[pl.ds(i * 15, 15)], sem.at[i])
+        for i in range(4)
+    ]
+    for store in stores:
+        store.start()
     values = spread(recv_o)
     sel = (iota((8, COLS), 1) == LEVC).astype(F32).astype(BF16)
     power = dot_nt(sel, values[1])
@@ -512,9 +557,10 @@
     node[0] = tend_w * (1.0 / SCALE_T)
     node[1] = (tend_ref[...] - tend_w) * (1.0 / SCALE_Q)
     node[2] = refine(fine_ref, 1, node_o) * (1.0 / SCALE_Q)
-    close = pltpu.make_async_copy(node, node_out, sem.at[1])
+    close = pltpu.make_async_copy(node, node_out, sem.at[4])
     close.start()
-    store.wait()
+    for store in stores:
+        store.wait()
     close.wait()
 
 
@@ -523,6 +569,9 @@
 
     def body(gcm, place, switch, cmap, pert_temp, pert_moist, fmap, node_ids, weight):
         hbm = pl.BlockSpec(memory_space=pltpu.HBM)
+        n = n_sec * n_col
+        states = pltpu.VMEM((n * PIECES, 2 * COLS // n, COLS), BF16)
+        entries = pltpu.VMEM((n, ROWS // n, COLS), jnp.int16)
         field = pltpu.VMEM((LEVC + 2, CRMX, COLS), F32)
         plane = pltpu.VMEM((64, COLS), F32)
         vmem = pl.BlockSpec(memory_space=pltpu.VMEM)
@@ -530,7 +579,7 @@
             functools.partial(kernel, n_sec, n_col),
             out_shape=(
                 pltpu.VMEM((LEVC, CRMX, COLS), BF16),
-                pltpu.VMEM((ROWS, COLS), jnp.int16),
+                pltpu.VMEM((n, ROWS // n, COLS), jnp.int16),
                 pltpu.VMEM((8, ROWS), F32),
                 pltpu.VMEM((LEV, COLS), F32),
                 pltpu.VMEM((COLS, COLS), F32),
@@ -551,16 +600,17 @@
                 field,
                 field,
                 field,
-                pltpu.VMEM((COLS, 4 * COLS), BF16),
-                pltpu.VMEM((ROWS, COLS), BF16),
-                pltpu.VMEM((ROWS, COLS), BF16),
+                pltpu.VMEM((COLS, PIECES * COLS), BF16),
+                states,
+                states,
                 pltpu.VMEM((ROWS, COLS), BF16),
                 pltpu.VMEM((ROWS, COLS), F32),
                 pltpu.VMEM((ROWS, COLS), F32),
-                pltpu.VMEM((ROWS, COLS), jnp.int16),
-                pltpu.VMEM((ROWS, COLS), jnp.int16),
-                pltpu.VMEM((ROWS, COLS), jnp.int16),
-                pltpu.VMEM((64, COLS), BF16),
+                entries,
+                entries,
+                entries,
+                pltpu.VMEM((COLS, 2 * COLS), BF16),
+                pltpu.VMEM((4 * 64, PIECES * COLS), BF16),
                 pltpu.VMEM((COLS, COLS), F32),
             ]
             + [plane] * 11
@@ -595,7 +645,7 @@
             out_specs=(hbm, hbm),
             scratch_shapes=[
                 pltpu.VMEM((3, LEV, COLS), F32),
-                pltpu.SemaphoreType.DMA((2,)),
+                pltpu.SemaphoreType.DMA((5,)),
             ],
             compiler_params=pltpu.CompilerParams(vmem_limit_bytes=8 * 1024 * 1024),
             name="sum_on_nodes",

time: 39.5 us -> 38 us (0.962)
  Pallas kernels: 38.8 us -> 37.3 us
    pallas_call x1, Pallas kernels: 37.3 us -> 35.8 us  [body(): pl.pallas_call(functools.partial(kernel, n_sec, n_col), out_shape=(pltpu....]
where the time goes in v4:
time: 38 us; the launch traced here: 37.9 us
  Pallas kernels  37.3 us (98%)
  between operations  0.64 us (2%)
    pallas_call x1, Pallas kernels, body(): pl.pallas_call(functools.partial(kernel, n_sec, n_col), out_shape=(pltpu....  35.8 us
    pallas_call x1, Pallas kernels, body(): pl.pallas_call(finish, out_shape=(jax.ShapeDtypeStruct((LEVC, CRMX, COLS)...  1.48 us

profile of v4, /device:TPU:1, one launch (start us, length us, event | category | flops | bytes accessed | tf_op | source)
XLA Modules:
  0.0 37.9 jit_solution(6035776248897426651)
XLA Ops:
  0.6 35.8 %physics_step.1 = (bf16[60,64,128]{2,1,0:T(8,128)(2,1)S(1)}, s16[128,8,128]{2,1,0:T(8,128)(2,1)S(1)}, f32[8,1024]{1,0:T(8,128)S(1)}, f32[72,128]{1,0:T(8,128)S(1)}, f32[128,128]{1,0:T(8,128)S(1)}) custom-call(bf16[4,72,128]{2,1,0:T(8,128)(2,1)} %gcm_hbm.1, s32[1,128]{1,0:T(1,128)} %bitcast.4, s32[1,128]{1,0:T(1,128)} %bitcast.5, bf16[60,72]{1,0:T(8,128)(2,1)} %cmap_hbm.1, ...), custom_call_target="tpu_custom_call" | custom-call | tf_op jit(solution)/shard_map/physics_step/pallas_call | solution.py:578
  36.5 1.5 %sum_on_nodes.1 = (bf16[60,64,128]{2,1,0:T(8,128)(2,1)}, f32[3,72,128]{2,1,0:T(8,128)}) custom-call(bf16[60,64,128]{2,1,0:T(8,128)(2,1)S(1)} %get-tuple-element.7.crm, s16[128,8,128]{2,1,0:T(8,128)(2,1)S(1)} %get-tuple-element.8.recv_o, f32[8,1024]{1,0:T(8,128)S(1)} %get-tuple-element.9.codes_ref, f32[72,128]{1,0:T(8,128)S(1)} %get-tuple-element.10.tend_ref, ...), custom_call_target="tpu_custom_call" | custom-call | tf_op jit(solution)/shard_map/sum_on_nodes/pallas_call | solution.py:638

commit v5 on v4

--- a/solution.py
+++ b/solution.py
@@ -107,7 +107,8 @@
     fpad,
     c_bx,
     c_cx,
-    c_a,
+    c_scale,
+    c_over,
     c_b,
     c_cz,
     c_arg,
@@ -140,15 +141,16 @@
 
     def each_peer(act):
         def plane(t):
-            x = wrap(wrap(my_x + 2 + lax.div(t, 4)))
-            z = wrap(wrap(my_z + 2 + lax.rem(t, 4)))
+            ta = lax.div(t, 4)
+            x = wrap(wrap(my_x + 2 + ta))
+            z = wrap(wrap(my_z + 2 + wrap(lax.rem(t, 4) + ta)))
             base = x * 16 + z * 4
             for y in ys:
                 col = base + y
                 for sec in secs:
                     if y is ys[3] and sec is my_sec:
 
-                        @pl.when(t != 10)
+                        @pl.when(t != 8)
                         def _():
                             act(sec * n_col + col, (sec, col))
 
@@ -374,8 +376,15 @@
     c_bx[...] = jnp.abs(cx) / keep
     c_cx[...] = cx
     c_cz[...] = cz
-    c_a[...] = (1.0 - az) * keep
-    c_b[...] = az * jnp.where(from_below, below(keep), above(keep))
+    shrink = (1.0 - az) * keep
+    log_shrink = jnp.log2(shrink)
+    scale = jnp.ones_like(keep)
+    for sub in range(SUB):
+        before = scale * keep
+        scale = scale * shrink
+        c_scale[sub] = scale
+        c_over[sub] = 1.0 / scale
+        c_b[sub] = az * jnp.where(from_below, below(before), above(before)) / scale
 
     def lift(x):
         return x - az * (x - jnp.where(from_below, below(x), above(x)))
@@ -421,16 +430,12 @@
     pack_n = pack_nodes(change_n, jnp.zeros_like(change_n), send_n, True)
     pack_n(STEPS, 64)
 
-    def first_x(k, carry):
-        here = pl.ds(k, 1)
-        bx = c_bx[here, :]
-        up = jnp.broadcast_to(c_cx[here, :] > 0.0, (CRMX, COLS))
-        for src, dst in ((wb, wa), (qb, qa)):
-            g = src[k + 1]
-            dst[k + 1] = g + bx * jnp.where(up, left(g), right(g))
-        return carry
-
-    lax.fori_loop(0, LEVC, first_x, 0)
+    def along_x(g, k):
+        up = jnp.broadcast_to(c_cx[pl.ds(k, 1), :] > 0.0, (CRMX, COLS))
+        return g + c_bx[pl.ds(k, 1), :] * jnp.where(up, left(g), right(g))
+
+    for ref in (wb, qb):
+        ref[1] = along_x(ref[1], 0)
 
     half = 0.5 * flag
     mean_w, mean_q = start_w, start_q
@@ -438,7 +443,7 @@
     cond = jnp.zeros_like(mean_w)
     for sub in range(SUB):
         last = sub == SUB - 1
-        source, sink = ((wa, qa), (wb, qb)) if sub % 2 == 0 else ((wb, qb), (wa, qa))
+        source, sink = ((wb, qb), (wa, qa)) if sub % 2 == 0 else ((wa, qa), (wb, qb))
         lifted = lift(mean_w)
         relax = 0.3 * (goal_w - lifted)
         mean_w = lifted + relax
@@ -447,11 +452,11 @@
         relax = 0.3 * (goal_q - lifted)
         mean_q = lifted + relax
         off_q = lift(off_q) + relax
-        c_arg[...] = off_w + LOG_CAPACITY
-        c_neg[...] = -off_q
+        c_arg[...] = off_w + (LOG_CAPACITY - (sub + 1) * log_shrink)
+        c_neg[...] = -off_q * c_over[sub]
         off_w = off_w + half * off_q
         if last:
-            c_fin[...] = off_w
+            c_fin[...] = off_w * (1.0 / SCALE_T)
 
         def step(it, carry, source=source, sink=sink, last=last, sub=sub):
             k0 = it * UNROLL
@@ -461,31 +466,35 @@
                 push_n(it)
             w_rows = [source[0][k0 + u] for u in range(UNROLL + 2)]
             q_rows = [source[1][k0 + u] for u in range(UNROLL + 2)]
+            if sub == 0:
+                for ref, group in zip(source, (w_rows, q_rows)):
+                    for u in range(2, UNROLL + 2):
+                        group[u] = along_x(group[u], k0 + u - 1)
+                        if u >= UNROLL:
+                            ref[k0 + u] = group[u]
             for u in range(UNROLL):
                 here = pl.ds(k0 + u, 1)
-                a, b = c_a[here, :], c_b[here, :]
+                b, scale = c_b[sub, here, :], c_scale[sub, here, :]
                 down = jnp.broadcast_to(c_cz[here, :] > 0.0, (CRMX, COLS))
-                w = a * w_rows[u + 1] + b * jnp.where(down, w_rows[u], w_rows[u + 2])
-                q = a * q_rows[u + 1] + b * jnp.where(down, q_rows[u], q_rows[u + 2])
-                gain = jnp.maximum(q - jnp.exp2(w + c_arg[here, :]), c_neg[here, :])
+                w = w_rows[u + 1] + b * jnp.where(down, w_rows[u], w_rows[u + 2])
+                q = q_rows[u + 1] + b * jnp.where(down, q_rows[u], q_rows[u + 2])
+                over = q - jnp.exp2(scale * w + c_arg[here, :])
+                gain = jnp.maximum(over, c_neg[here, :])
                 c_sum[here, :] = jnp.sum(gain, axis=0, keepdims=True)
                 gain = half * gain
                 w = w + gain
                 if last:
                     sink[0][k0 + u + 1] = w
                 else:
-                    q = q - gain
-                    bx = c_bx[here, :]
-                    up = jnp.broadcast_to(c_cx[here, :] > 0.0, (CRMX, COLS))
-                    sink[0][k0 + u + 1] = w + bx * jnp.where(up, left(w), right(w))
-                    sink[1][k0 + u + 1] = q + bx * jnp.where(up, left(q), right(q))
+                    sink[0][k0 + u + 1] = along_x(w, k0 + u)
+                    sink[1][k0 + u + 1] = along_x(q - gain, k0 + u)
             return carry
 
         if sub == 1:
             own_n, push_n = exchange(send_n, recv_n, 1)
             push_n(STEPS)
         lax.fori_loop(0, STEPS, step, 0)
-        added = half * (c_sum[...] * (1.0 / CRMX) + off_q)
+        added = half * (c_sum[...] * c_scale[sub] * (1.0 / CRMX) + off_q)
         off_q = off_q - half * off_q
         mean_w = mean_w + added
         mean_q = mean_q - added
@@ -499,7 +508,9 @@
     def close_rows(it, carry):
         for u in range(4):
             k = it * 4 + u
-            t = ((wa[k + 1] + c_fin[pl.ds(k, 1), :]) * (1.0 / SCALE_T)).astype(BF16)
+            here = pl.ds(k, 1)
+            t = wb[k + 1] * (c_scale[SUB - 1, here, :] * (1.0 / SCALE_T)) + c_fin[here, :]
+            t = t.astype(BF16)
             crm[k] = dot_nn(regroup, t).astype(BF16)
         return carry
 
@@ -574,6 +585,7 @@
         entries = pltpu.VMEM((n, ROWS // n, COLS), jnp.int16)
         field = pltpu.VMEM((LEVC + 2, CRMX, COLS), F32)
         plane = pltpu.VMEM((64, COLS), F32)
+        planes = pltpu.VMEM((SUB, 64, COLS), F32)
         vmem = pl.BlockSpec(memory_space=pltpu.VMEM)
         between = pl.pallas_call(
             functools.partial(kernel, n_sec, n_col),
@@ -613,7 +625,9 @@
                 pltpu.VMEM((4 * 64, PIECES * COLS), BF16),
                 pltpu.VMEM((COLS, COLS), F32),
             ]
-            + [plane] * 11
+            + [plane] * 2
+            + [planes] * 3
+            + [plane] * 7
             + [
                 pltpu.SemaphoreType.DMA((9,)),
                 pltpu.SemaphoreType.DMA((3,)),

time: 38 us -> 37.2 us (0.979)
  Pallas kernels: 37.3 us -> 36.4 us
    pallas_call x1, Pallas kernels: 35.8 us -> 34.9 us  [body(): pl.pallas_call(functools.partial(kernel, n_sec, n_col), out_shape=(pltpu....]
where the time goes in v5:
time: 37.2 us; the launch traced here: 37 us
  Pallas kernels  36.4 us (98%)
  between operations  0.64 us (2%)
    pallas_call x1, Pallas kernels, body(): pl.pallas_call(functools.partial(kernel, n_sec, n_col), out_shape=(pltpu....  34.9 us
    pallas_call x1, Pallas kernels, body(): pl.pallas_call(finish, out_shape=(jax.ShapeDtypeStruct((LEVC, CRMX, COLS)...  1.48 us

profile of v5, /device:TPU:1, one launch (start us, length us, event | category | flops | bytes accessed | tf_op | source)
XLA Modules:
  0.0 37.0 jit_solution(17202484349235217392)
XLA Ops:
  0.6 34.9 %physics_step.1 = (bf16[60,64,128]{2,1,0:T(8,128)(2,1)S(1)}, s16[128,8,128]{2,1,0:T(8,128)(2,1)S(1)}, f32[8,1024]{1,0:T(8,128)S(1)}, f32[72,128]{1,0:T(8,128)S(1)}, f32[128,128]{1,0:T(8,128)S(1)}) custom-call(bf16[4,72,128]{2,1,0:T(8,128)(2,1)} %gcm_hbm.1, s32[1,128]{1,0:T(1,128)} %bitcast.4, s32[1,128]{1,0:T(1,128)} %bitcast.5, bf16[60,72]{1,0:T(8,128)(2,1)} %cmap_hbm.1, ...), custom_call_target="tpu_custom_call" | custom-call | tf_op jit(solution)/shard_map/physics_step/pallas_call | solution.py:590
  35.6 1.5 %sum_on_nodes.1 = (bf16[60,64,128]{2,1,0:T(8,128)(2,1)}, f32[3,72,128]{2,1,0:T(8,128)}) custom-call(bf16[60,64,128]{2,1,0:T(8,128)(2,1)S(1)} %get-tuple-element.7.crm, s16[128,8,128]{2,1,0:T(8,128)(2,1)S(1)} %get-tuple-element.8.recv_o, f32[8,1024]{1,0:T(8,128)S(1)} %get-tuple-element.9.codes_ref, f32[72,128]{1,0:T(8,128)S(1)} %get-tuple-element.10.tend_ref, ...), custom_call_target="tpu_custom_call" | custom-call | tf_op jit(solution)/shard_map/sum_on_nodes/pallas_call | solution.py:652

commit v6 on v5

--- a/solution.py
+++ b/solution.py
@@ -100,6 +100,7 @@
     slot_gain,
     slot_code,
     send_n,
+    relay,
     recv_n,
     send_o,
     halves,
@@ -437,6 +438,19 @@
     for ref in (wb, qb):
         ref[1] = along_x(ref[1], 0)
 
+    def push_relay(step):
+        col = my_col + step
+        col = jnp.where(col >= n_col, col - n_col, col)
+        pltpu.make_async_remote_copy(
+            src_ref=send_n.at[:, col],
+            dst_ref=relay.at[:, my_col],
+            send_sem=tx_sem.at[1],
+            recv_sem=rx_sem.at[1],
+            device_id=(my_sec, col),
+            device_id_type=MESH,
+        ).start()
+
+    relays = (n_col - 1) // STEPS
     half = 0.5 * flag
     mean_w, mean_q = start_w, start_q
     off_w, off_q = goal_w, goal_q
@@ -463,7 +477,8 @@
             if sub == 0:
                 pack_n(it, 64)
             if sub == 1:
-                push_n(it)
+                for u in range(relays):
+                    push_relay(it * relays + (u + 1))
             w_rows = [source[0][k0 + u] for u in range(UNROLL + 2)]
             q_rows = [source[1][k0 + u] for u in range(UNROLL + 2)]
             if sub == 0:
@@ -491,8 +506,10 @@
             return carry
 
         if sub == 1:
-            own_n, push_n = exchange(send_n, recv_n, 1)
-            push_n(STEPS)
+            own_n = pltpu.make_async_copy(send_n.at[:, my_col], relay.at[:, my_col], own_sem.at[1])
+            own_n.start()
+            for hop in range(relays * STEPS + 1, n_col):
+                push_relay(hop)
         lax.fori_loop(0, STEPS, step, 0)
         added = half * (c_sum[...] * c_scale[sub] * (1.0 / CRMX) + off_q)
         off_q = off_q - half * off_q
@@ -516,7 +533,27 @@
 
     lax.fori_loop(0, LEVC // 4, close_rows, 0)
     own_n.wait()
-    all_of(send_n, recv_n, 1).wait_recv()
+    pltpu.make_async_remote_copy(
+        src_ref=send_n.at[:, pl.ds(0, n_col - 1)],
+        dst_ref=relay.at[:, pl.ds(0, n_col - 1)],
+        send_sem=tx_sem.at[1],
+        recv_sem=rx_sem.at[1],
+        device_id=(1 - my_sec, my_col),
+        device_id_type=MESH,
+    ).wait()
+    keep_n = pltpu.make_async_copy(relay.at[my_sec], recv_n.at[my_sec], own_sem.at[1])
+    keep_n.start()
+    cross = pltpu.make_async_remote_copy(
+        src_ref=relay.at[1 - my_sec],
+        dst_ref=recv_n.at[my_sec],
+        send_sem=tx_sem.at[3],
+        recv_sem=rx_sem.at[3],
+        device_id=(1 - my_sec, my_col),
+        device_id_type=MESH,
+    )
+    cross.start()
+    keep_n.wait()
+    cross.wait()
 
     values_n = spread(recv_n)
     sel = (lane8 == LEVC + iota((8, COLS), 0)).astype(F32).astype(BF16)
@@ -525,7 +562,6 @@
     fine_ref[...] = fpad[...].T
     tend_ref[...] = refine(fine_ref, 0, node_n)
     all_of(send_s, recv_s, 0).wait_send()
-    all_of(send_n, recv_n, 1).wait_send()
     own_o.wait()
     all_of(send_o, recv_o, 2).wait()
 
@@ -582,6 +618,7 @@
         hbm = pl.BlockSpec(memory_space=pltpu.HBM)
         n = n_sec * n_col
         states = pltpu.VMEM((n * PIECES, 2 * COLS // n, COLS), BF16)
+        by_chip = pltpu.VMEM((n_sec, n_col, ROWS // n, COLS), jnp.int16)
         entries = pltpu.VMEM((n, ROWS // n, COLS), jnp.int16)
         field = pltpu.VMEM((LEVC + 2, CRMX, COLS), F32)
         plane = pltpu.VMEM((64, COLS), F32)
@@ -618,8 +655,9 @@
                 pltpu.VMEM((ROWS, COLS), BF16),
                 pltpu.VMEM((ROWS, COLS), F32),
                 pltpu.VMEM((ROWS, COLS), F32),
-                entries,
-                entries,
+                by_chip,
+                by_chip,
+                by_chip,
                 entries,
                 pltpu.VMEM((COLS, 2 * COLS), BF16),
                 pltpu.VMEM((4 * 64, PIECES * COLS), BF16),
@@ -631,8 +669,8 @@
             + [
                 pltpu.SemaphoreType.DMA((9,)),
                 pltpu.SemaphoreType.DMA((3,)),
-                pltpu.SemaphoreType.DMA((3,)),
-                pltpu.SemaphoreType.DMA((3,)),
+                pltpu.SemaphoreType.DMA((4,)),
+                pltpu.SemaphoreType.DMA((4,)),
             ],
             compiler_params=pltpu.CompilerParams(
                 collective_id=0, has_side_effects=True, vmem_limit_bytes=65000000

time: 37.2 us -> 36.7 us (0.987)
  Pallas kernels: 36.4 us -> 35.9 us
    pallas_call x1, Pallas kernels: 34.9 us -> 34.5 us  [body(): pl.pallas_call(functools.partial(kernel, n_sec, n_col), out_shape=(pltpu....]
where the time goes in v6:
time: 36.7 us; the launch traced here: 36.6 us
  Pallas kernels  35.9 us (98%)
  between operations  0.64 us (2%)
    pallas_call x1, Pallas kernels, body(): pl.pallas_call(functools.partial(kernel, n_sec, n_col), out_shape=(pltpu....  34.5 us
    pallas_call x1, Pallas kernels, body(): pl.pallas_call(finish, out_shape=(jax.ShapeDtypeStruct((LEVC, CRMX, COLS)...  1.48 us

profile of v6, /device:TPU:1, one launch (start us, length us, event | category | flops | bytes accessed | tf_op | source)
XLA Modules:
  0.0 36.6 jit_solution(184419400025624547)
XLA Ops:
  0.6 34.5 %physics_step.1 = (bf16[60,64,128]{2,1,0:T(8,128)(2,1)S(1)}, s16[128,8,128]{2,1,0:T(8,128)(2,1)S(1)}, f32[8,1024]{1,0:T(8,128)S(1)}, f32[72,128]{1,0:T(8,128)S(1)}, f32[128,128]{1,0:T(8,128)S(1)}) custom-call(bf16[4,72,128]{2,1,0:T(8,128)(2,1)} %gcm_hbm.1, s32[1,128]{1,0:T(1,128)} %bitcast.4, s32[1,128]{1,0:T(1,128)} %bitcast.5, bf16[60,72]{1,0:T(8,128)(2,1)} %cmap_hbm.1, ...), custom_call_target="tpu_custom_call" | custom-call | tf_op jit(solution)/shard_map/physics_step/pallas_call | solution.py:627
  35.1 1.5 %sum_on_nodes.1 = (bf16[60,64,128]{2,1,0:T(8,128)(2,1)}, f32[3,72,128]{2,1,0:T(8,128)}) custom-call(bf16[60,64,128]{2,1,0:T(8,128)(2,1)S(1)} %get-tuple-element.7.crm, s16[128,8,128]{2,1,0:T(8,128)(2,1)S(1)} %get-tuple-element.8.recv_o, f32[8,1024]{1,0:T(8,128)S(1)} %get-tuple-element.9.codes_ref, f32[72,128]{1,0:T(8,128)S(1)} %get-tuple-element.10.tend_ref, ...), custom_call_target="tpu_custom_call" | custom-call | tf_op jit(solution)/shard_map/sum_on_nodes/pallas_call | solution.py:690

commit v7 on v6

--- a/solution.py
+++ b/solution.py
@@ -16,8 +16,8 @@
 ROWS = 1024
 TAIL = 4 * LEV - 2 * COLS
 PIECES = 3
-UNROLL = 4
-STEPS = LEVC // UNROLL
+UNROLL = (4, 4, 6, 6)
+STEPS = LEVC // UNROLL[0]
 SCALE_T = 0.3 * math.log2(math.e)
 SCALE_Q = 1.5 * SCALE_T
 LOG_CAPACITY = math.log2(0.5 * SCALE_Q)
@@ -472,22 +472,24 @@
         if last:
             c_fin[...] = off_w * (1.0 / SCALE_T)
 
-        def step(it, carry, source=source, sink=sink, last=last, sub=sub):
-            k0 = it * UNROLL
+        unroll = UNROLL[sub]
+
+        def step(it, carry, source=source, sink=sink, last=last, sub=sub, unroll=unroll):
+            k0 = it * unroll
             if sub == 0:
                 pack_n(it, 64)
             if sub == 1:
                 for u in range(relays):
                     push_relay(it * relays + (u + 1))
-            w_rows = [source[0][k0 + u] for u in range(UNROLL + 2)]
-            q_rows = [source[1][k0 + u] for u in range(UNROLL + 2)]
+            w_rows = [source[0][k0 + u] for u in range(unroll + 2)]
+            q_rows = [source[1][k0 + u] for u in range(unroll + 2)]
             if sub == 0:
                 for ref, group in zip(source, (w_rows, q_rows)):
-                    for u in range(2, UNROLL + 2):
+                    for u in range(2, unroll + 2):
                         group[u] = along_x(group[u], k0 + u - 1)
-                        if u >= UNROLL:
+                        if u >= unroll:
                             ref[k0 + u] = group[u]
-            for u in range(UNROLL):
+            for u in range(unroll):
                 here = pl.ds(k0 + u, 1)
                 b, scale = c_b[sub, here, :], c_scale[sub, here, :]
                 down = jnp.broadcast_to(c_cz[here, :] > 0.0, (CRMX, COLS))
@@ -510,7 +512,7 @@
             own_n.start()
             for hop in range(relays * STEPS + 1, n_col):
                 push_relay(hop)
-        lax.fori_loop(0, STEPS, step, 0)
+        lax.fori_loop(0, LEVC // unroll, step, 0)
         added = half * (c_sum[...] * c_scale[sub] * (1.0 / CRMX) + off_q)
         off_q = off_q - half * off_q
         mean_w = mean_w + added
@@ -518,7 +520,7 @@
         cond = cond + added
 
     pack_o = pack_nodes(mean_w - start_w, cond, send_o, False)
-    repeat(lambda i: pack_o(i, 256), 0, ROWS // 256)
+    pack_o(0, ROWS)
     own_o, push_o = exchange(send_o, recv_o, 2)
     repeat(push_o, 0, 16)
 

time: 36.7 us -> 36.1 us (0.984)
  Pallas kernels: 35.9 us -> 35.3 us
    pallas_call x1, Pallas kernels: 34.5 us -> 33.9 us  [body(): pl.pallas_call(functools.partial(kernel, n_sec, n_col), out_shape=(pltpu....]
where the time goes in v7:
time: 36.1 us; the launch traced here: 36 us
  Pallas kernels  35.3 us (98%)
  between operations  0.64 us (2%)
    pallas_call x1, Pallas kernels, body(): pl.pallas_call(functools.partial(kernel, n_sec, n_col), out_shape=(pltpu....  33.9 us
    pallas_call x1, Pallas kernels, body(): pl.pallas_call(finish, out_shape=(jax.ShapeDtypeStruct((LEVC, CRMX, COLS)...  1.48 us

profile of v7, /device:TPU:1, one launch (start us, length us, event | category | flops | bytes accessed | tf_op | source)
XLA Modules:
  0.0 36.0 jit_solution(13802792633127360069)
XLA Ops:
  0.6 33.9 %physics_step.1 = (bf16[60,64,128]{2,1,0:T(8,128)(2,1)S(1)}, s16[128,8,128]{2,1,0:T(8,128)(2,1)S(1)}, f32[8,1024]{1,0:T(8,128)S(1)}, f32[72,128]{1,0:T(8,128)S(1)}, f32[128,128]{1,0:T(8,128)S(1)}) custom-call(bf16[4,72,128]{2,1,0:T(8,128)(2,1)} %gcm_hbm.1, s32[1,128]{1,0:T(1,128)} %bitcast.4, s32[1,128]{1,0:T(1,128)} %bitcast.5, bf16[60,72]{1,0:T(8,128)(2,1)} %cmap_hbm.1, ...), custom_call_target="tpu_custom_call" | custom-call | tf_op jit(solution)/shard_map/physics_step/pallas_call | solution.py:629
  34.5 1.5 %sum_on_nodes.1 = (bf16[60,64,128]{2,1,0:T(8,128)(2,1)}, f32[3,72,128]{2,1,0:T(8,128)}) custom-call(bf16[60,64,128]{2,1,0:T(8,128)(2,1)S(1)} %get-tuple-element.7.crm, s16[128,8,128]{2,1,0:T(8,128)(2,1)S(1)} %get-tuple-element.8.recv_o, f32[8,1024]{1,0:T(8,128)S(1)} %get-tuple-element.9.codes_ref, f32[72,128]{1,0:T(8,128)S(1)} %get-tuple-element.10.tend_ref, ...), custom_call_target="tpu_custom_call" | custom-call | tf_op jit(solution)/shard_map/sum_on_nodes/pallas_call | solution.py:692

commit v8 on v7

--- a/solution.py
+++ b/solution.py
@@ -359,11 +359,12 @@
     hot = (labels == target).astype(F32).astype(BF16)
     period = PIECES * 16
     piece = lax.rem(iota((period, COLS), 0), PIECES * cap) // cap
-    placed = []
-    for f in range(PIECES):
-        mine = jnp.tile((piece == f).astype(F32).astype(BF16), (span_s // period, 1)) * arrived
-        placed.append(dot_nn(hot, mine).astype(BF16))
-    profiles = dot_nt(cpad[...], jnp.concatenate(placed, axis=1))
+    mine = [
+        jnp.tile((piece == f).astype(F32).astype(BF16), (span_s // period, 1)) * arrived
+        for f in range(PIECES)
+    ]
+    placed = dot_nn(hot, jnp.concatenate(mine, axis=1)).astype(BF16)
+    profiles = dot_nt(cpad[...], placed)
     profile = [profiles[v * 64 : (v + 1) * 64] for v in range(4)]
     flag = profile[0][LEVC : LEVC + 1, :]
 

time: 36.1 us -> 36.1 us (level)
  no operation moved by 1% of the time
where the time goes in v8:
time: 36.1 us; the launch traced here: 35.9 us
  Pallas kernels  35.3 us (98%)
  between operations  0.64 us (2%)
    pallas_call x1, Pallas kernels, body(): pl.pallas_call(functools.partial(kernel, n_sec, n_col), out_shape=(pltpu....  33.8 us
    pallas_call x1, Pallas kernels, body(): pl.pallas_call(finish, out_shape=(jax.ShapeDtypeStruct((LEVC, CRMX, COLS)...  1.48 us

profile of v8, /device:TPU:1, one launch (start us, length us, event | category | flops | bytes accessed | tf_op | source)
XLA Modules:
  0.0 35.9 jit_solution(13730523148608000208)
XLA Ops:
  0.6 33.8 %physics_step.1 = (bf16[60,64,128]{2,1,0:T(8,128)(2,1)S(1)}, s16[128,8,128]{2,1,0:T(8,128)(2,1)S(1)}, f32[8,1024]{1,0:T(8,128)S(1)}, f32[72,128]{1,0:T(8,128)S(1)}, f32[128,128]{1,0:T(8,128)S(1)}) custom-call(bf16[4,72,128]{2,1,0:T(8,128)(2,1)} %gcm_hbm.1, s32[1,128]{1,0:T(1,128)} %bitcast.4, s32[1,128]{1,0:T(1,128)} %bitcast.5, bf16[60,72]{1,0:T(8,128)(2,1)} %cmap_hbm.1, ...), custom_call_target="tpu_custom_call" | custom-call | tf_op jit(solution)/shard_map/physics_step/pallas_call | solution.py:630
  34.5 1.5 %sum_on_nodes.1 = (bf16[60,64,128]{2,1,0:T(8,128)(2,1)}, f32[3,72,128]{2,1,0:T(8,128)}) custom-call(bf16[60,64,128]{2,1,0:T(8,128)(2,1)S(1)} %get-tuple-element.7.crm, s16[128,8,128]{2,1,0:T(8,128)(2,1)S(1)} %get-tuple-element.8.recv_o, f32[8,1024]{1,0:T(8,128)S(1)} %get-tuple-element.9.codes_ref, f32[72,128]{1,0:T(8,128)S(1)} %get-tuple-element.10.tend_ref, ...), custom_call_target="tpu_custom_call" | custom-call | tf_op jit(solution)/shard_map/sum_on_nodes/pallas_call | solution.py:693

commit v9 on v8

--- a/solution.py
+++ b/solution.py
@@ -256,16 +256,18 @@
     tail = jnp.where(at == 0, label, jnp.where(at == 1, flag_in, 0.0))
     ext[TAIL:COLS, 2 * COLS : 3 * COLS] = tail.astype(BF16)
 
+    half_s = span_s // 2
+
     def pack_state(chunk):
-        row = iota((COLS, COLS), 0) + chunk * COLS
+        row = iota((half_s, COLS), 0) + chunk * half_s
         hot = jnp.concatenate(
             [(row == slot + f * cap).astype(F32).astype(BF16) for f in range(PIECES)], axis=1
         )
-        send_rows[pl.ds(pl.multiple_of(chunk * COLS, COLS), COLS), :] = dot_nt(
+        send_rows[pl.ds(pl.multiple_of(chunk * half_s, half_s), half_s), :] = dot_nt(
             hot, ext[...]
         ).astype(BF16)
 
-    repeat(pack_state, 0, span_s // COLS)
+    repeat(pack_state, 0, 2)
 
     pl.semaphore_wait(barrier, n - 1)
     own_s, push_s = exchange(send_s, recv_s, 0)

time: 36.1 us -> 36.1 us (level)
  no operation moved by 1% of the time
where the time goes in v9:
time: 36.1 us; the launch traced here: 35.9 us
  Pallas kernels  35.3 us (98%)
  between operations  0.64 us (2%)
    pallas_call x1, Pallas kernels, body(): pl.pallas_call(functools.partial(kernel, n_sec, n_col), out_shape=(pltpu....  33.8 us
    pallas_call x1, Pallas kernels, body(): pl.pallas_call(finish, out_shape=(jax.ShapeDtypeStruct((LEVC, CRMX, COLS)...  1.48 us

profile of v9, /device:TPU:1, one launch (start us, length us, event | category | flops | bytes accessed | tf_op | source)
XLA Modules:
  0.0 35.9 jit_solution(13457871749534051209)
XLA Ops:
  0.6 33.8 %physics_step.1 = (bf16[60,64,128]{2,1,0:T(8,128)(2,1)S(1)}, s16[128,8,128]{2,1,0:T(8,128)(2,1)S(1)}, f32[8,1024]{1,0:T(8,128)S(1)}, f32[72,128]{1,0:T(8,128)S(1)}, f32[128,128]{1,0:T(8,128)S(1)}) custom-call(bf16[4,72,128]{2,1,0:T(8,128)(2,1)} %gcm_hbm.1, s32[1,128]{1,0:T(1,128)} %bitcast.4, s32[1,128]{1,0:T(1,128)} %bitcast.5, bf16[60,72]{1,0:T(8,128)(2,1)} %cmap_hbm.1, ...), custom_call_target="tpu_custom_call" | custom-call | tf_op jit(solution)/shard_map/physics_step/pallas_call | solution.py:632
  34.5 1.5 %sum_on_nodes.1 = (bf16[60,64,128]{2,1,0:T(8,128)(2,1)}, f32[3,72,128]{2,1,0:T(8,128)}) custom-call(bf16[60,64,128]{2,1,0:T(8,128)(2,1)S(1)} %get-tuple-element.7.crm, s16[128,8,128]{2,1,0:T(8,128)(2,1)S(1)} %get-tuple-element.8.recv_o, f32[8,1024]{1,0:T(8,128)S(1)} %get-tuple-element.9.codes_ref, f32[72,128]{1,0:T(8,128)S(1)} %get-tuple-element.10.tend_ref, ...), custom_call_target="tpu_custom_call" | custom-call | tf_op jit(solution)/shard_map/sum_on_nodes/pallas_call | solution.py:695
